TPU v7x, 32 devices: a whole 2x2x4 slice. The times are simulated.
32 devices in a mesh: shard: 8 (over z, x), ctx: 4 (over y, core).
Axes of the slice: x: 2, y: 2, z: 4, core: 2. Of those that a mesh axis runs over, the one named last changes fastest.
Arguments:
- layer_input: bfloat16 [16, 256, 640], P('shard', 'ctx'), may hold values from -4 to 4
- out_cotangent: bfloat16 [16, 256, 640], P('shard', 'ctx'), may hold values from -6 to 6
- block_pairs: int32 [16, 4], P('shard'), may hold values from 0 to 3, each once within a row
- w_query: bfloat16 [640, 1024], P(None, 'shard'), may hold values from -0.0625 to 0.0625
- w_key: bfloat16 [640, 256], P(None, 'shard'), may hold values from -0.0625 to 0.0625
- w_value: bfloat16 [640, 256], P(None, 'shard'), may hold values from -0.25 to 0.25
- w_output: bfloat16 [1024, 640], P('shard'), may hold values from -0.1875 to 0.1875
- w_gate: bfloat16 [640, 2048], P(None, 'shard'), may hold values from -0.25 to 0.25
- w_up: bfloat16 [640, 2048], P(None, 'shard'), may hold values from -0.25 to 0.25
- w_down: bfloat16 [2048, 640], P('shard'), may hold values from -0.125 to 0.125
- input_gain: bfloat16 [640], P('shard'), may hold values from 0.099609375 to 1.8984375
- attnpost_gain: bfloat16 [640], P('shard'), may hold values from 0.099609375 to 1.8984375
- ffnpre_gain: bfloat16 [640], P('shard'), may hold values from 0.099609375 to 1.8984375
- ffnpost_gain: bfloat16 [640], P('shard'), may hold values from 0.099609375 to 1.8984375
- query_gain: bfloat16 [256], P('shard'), may hold values from 0.5 to 3
- key_gain: bfloat16 [256], P('shard'), may hold values from 0.5 to 3
Outputs:
- layer_output: bfloat16 [16, 256, 640], P('shard', 'ctx')
- input_grad: float32 [16, 256, 640], P('shard', 'ctx')
- wgrad_query: float32 [640, 1024], P(None, 'shard')
- wgrad_key: float32 [640, 256], P(None, 'shard')
- wgrad_value: float32 [640, 256], P(None, 'shard')
- wgrad_output: float32 [1024, 640], P('shard')
- wgrad_gate: float32 [640, 2048], P(None, 'shard')
- wgrad_up: float32 [640, 2048], P(None, 'shard')
- wgrad_down: float32 [2048, 640], P('shard')
- ggrad_input: float32 [640], P('shard')
- ggrad_attnpost: float32 [640], P('shard')
- ggrad_ffnpre: float32 [640], P('shard')
- ggrad_ffnpost: float32 [640], P('shard')
- ggrad_query: float32 [256], P('shard')
- ggrad_key: float32 [256], P('shard')
Inputs may be any that keep to these rules, and one draw needn't show every extreme that they name: Each row names every block pair once; context rank c holds blocks block_pairs[s, c] and 7 - block_pairs[s, c] of sequence s, in that order.
All inputs are finite; a program needn't handle non-finite values.
Results may differ from a plain program's by a relative error of at most 0.025.
The roundings to bfloat16 on the way count: a program that leaves them out, or rounds other values in their place, can miss the bound.
Values may be sent and summed in bfloat16 or wider, within the bound.
No kernel may reach another device: no remote copies, remote signals or barrier semaphores. Data moves between devices by JAX's collectives and lax.ppermute only.
A program may use at most 128 MiB of HBM per device.

v0:
```python
import functools

import jax
import jax.numpy as jnp
from jax import lax
from jax.experimental import pallas as pl
from jax.experimental.pallas import tpu as pltpu
from jax.sharding import PartitionSpec as P


epsilon = 1e-06
rope_base = 1000000.0
bf = jnp.bfloat16
f32 = jnp.float32
root = 0.7978845608028654
cubic = 0.044715


class Axis:
    def __init__(self, name):
        self.name = name
        self.size = lax.axis_size(name)
        assert self.size % 2 == 0
        self.inner = 2
        self.outer = self.size // 2
        self.rank = lax.axis_index(name)

    def send(self, x, d_outer, d_inner):
        n, m = self.outer, self.inner
        pairs = [
            (i, ((i // m + d_outer) % n) * m + (i % m + d_inner) % m) for i in range(self.size)
        ]
        return lax.ppermute(x, self.name, pairs)

    def shifts(self):
        return [(a, b) for a in range(self.outer) for b in range(self.inner)]

    def sources(self):
        n, m = self.outer, self.inner
        return [
            ((self.rank // m + n - a) % n) * m + (self.rank % m + m - b) % m
            for a, b in self.shifts()
        ]

    def gather(self, x):
        out = []
        for a in range(self.outer):
            far = self.send(x, a, 0) if a else x
            out += [far, self.send(far, 0, 1)]
        return out


def times(a, b):
    return lax.dot_general(a, b, (((1,), (0,)), ((), ())), preferred_element_type=f32)


def times_t(a, b):
    return lax.dot_general(a, b, (((1,), (1,)), ((), ())), preferred_element_type=f32)


def t_times(a, b):
    return lax.dot_general(a, b, (((0,), (0,)), ((), ())), preferred_element_type=f32)


def inverse_rms(v):
    return lax.rsqrt(jnp.mean(v * v, axis=-1, keepdims=True) + epsilon)


def norm(v, g):
    return v * inverse_rms(v) * g


def norm_back(v, g, dy):
    r = inverse_rms(v)
    gd = g * dy
    dv = r * gd - v * (r * r * r) * jnp.mean(v * gd, axis=-1, keepdims=True)
    return dv, jnp.sum(dy * v * r, axis=0, keepdims=True)


def call(body, outs, args, scalars=0, scratch=()):
    vmem = pl.BlockSpec(memory_space=pltpu.VMEM)
    smem = pl.BlockSpec(memory_space=pltpu.SMEM)
    return pl.pallas_call(
        body,
        out_shape=[jax.ShapeDtypeStruct(shape, kind) for shape, kind in outs],
        in_specs=[smem] * scalars + [vmem] * (len(args) - scalars),
        out_specs=[vmem] * len(outs),
        scratch_shapes=list(scratch),
    )(*args)


def rope_tables(positions, width):
    half = width // 2
    index = jnp.arange(half).astype(f32)
    freq = jnp.power(rope_base, -(2.0 * index) / width)
    angle = positions.astype(f32)[..., None] * freq
    return (jnp.cos(angle), jnp.sin(angle))


def seq_positions(pairs, blk):
    count = pairs.shape[-1]
    offset = jnp.arange(2 * blk, dtype=jnp.int32)
    chosen = pairs[..., None]
    block = jnp.where(offset < blk, chosen, 2 * count - 1 - chosen)
    return block * blk + offset % blk


def after(x, *deps):
    return lax.optimization_barrier((x,) + deps)[0]


def unpack(where, mine, other, piece, outs):
    count = len(mine)

    def put(low, high):
        for i in range(count):
            block = where[i]
            start = 0
            for out in outs:
                size = out.shape[0] // count
                for at, ref in ((0, low[i]), (piece, high[i])):
                    lo, hi = max(start, at), min(start + size, at + piece)
                    if lo < hi:
                        to = pl.multiple_of(block * size + (lo - start), 16)
                        out[pl.ds(to, hi - lo), :] = ref[lo - at : hi - at, :]
                start += size

    @pl.when(where[count] == 0)
    def _():
        put(mine, other)

    @pl.when(where[count] != 0)
    def _():
        put(other, mine)


def qkv_kernel(count, heads, where, x, cosine, sine, *refs):
    mine, other = refs[:count], refs[count : 2 * count]
    wq, wk, wv, gains, nin, qraw, kraw, qrot, kv = refs[2 * count :]
    piece = (wq.shape[0] + wk.shape[0] + wv.shape[0]) // count // 2
    hd = wk.shape[0]
    unpack(where, mine, other, piece, (wq, wk, wv))
    total = mine[0][piece:, :].astype(f32)
    for i in range(1, count):
        total = total + mine[i][piece:, :].astype(f32)
    gains[...] = total[: gains.shape[0], :]
    normed = norm(x[...].astype(f32), gains[0:1, :]).astype(bf)
    nin[...] = normed
    c, s = cosine[...], sine[...]
    half = hd // 2

    def turn(u):
        a, b = u[:, :half], u[:, half:]
        return a * c - b * s, b * c + a * s

    for h in range(heads):
        raw = times_t(normed, wq[h * hd : (h + 1) * hd, :])
        qraw[:, h * hd : (h + 1) * hd] = raw
        a, b = turn(norm(raw, gains[4:5, :hd]))
        qrot[:, h * hd : h * hd + half] = a.astype(bf)
        qrot[:, h * hd + half : (h + 1) * hd] = b.astype(bf)
    raw = times_t(normed, wk[...])
    kraw[...] = raw
    a, b = turn(norm(raw, gains[5:6, :hd]))
    kv[:, :half] = a.astype(bf)
    kv[:, half:hd] = b.astype(bf)
    kv[:, hd:] = times_t(normed, wv[...]).astype(bf)


def stacked(ref, rows, heads, hd):
    return jnp.concatenate([ref[rows, h * hd : (h + 1) * hd] for h in range(heads)], axis=0)


def attend_kernel(seqs, heads, scale, count, where, qpos, kpos, qrot, x, gains, *refs):
    mine, other, blocks = refs[:count], refs[count : 2 * count], refs[2 * count : -7]
    att, probs, kall, proj, resid, nmid, wo = refs[-7:]
    unpack(where, mine, other, mine[0].shape[0], (wo,))
    hd = kall.shape[1] // 2
    span = qrot.shape[0] // seqs
    length = len(blocks) * span
    for s in range(seqs):
        rows = slice(s * span, (s + 1) * span)
        for i, block in enumerate(blocks):
            kall[s * length + i * span : s * length + (i + 1) * span, :] = block[rows, :]
        keys = kall[s * length : (s + 1) * length, :hd]
        values = kall[s * length : (s + 1) * length, hd:]
        scores = times_t(stacked(qrot, rows, heads, hd), keys) * scale
        at = jnp.concatenate([qpos[rows, :]] * heads, axis=0)
        scores = jnp.where(kpos[s : s + 1, :] <= at, scores, -1e30)
        top = jnp.max(scores, axis=-1, keepdims=True)
        raised = jnp.exp(scores - top)
        p = raised / jnp.sum(raised, axis=-1, keepdims=True)
        probs[s * heads * span : (s + 1) * heads * span, :] = p
        out = times(p.astype(bf), values).astype(bf)
        for h in range(heads):
            att[rows, h * hd : (h + 1) * hd] = out[h * span : (h + 1) * span, :]
    projected = times(att[...], wo[...])
    proj[...] = projected
    r = x[...].astype(f32) + norm(projected, gains[1:2, :])
    resid[...] = r
    nmid[...] = norm(r, gains[2:3, :]).astype(bf)


def split(partial, count, keep, give):
    rows = partial.shape[0] // count
    for i in range(count):
        to = slice((i // 2) * rows, (i // 2 + 1) * rows)
        ref = give if i % 2 else keep
        ref[to, :] = partial[i * rows : (i + 1) * rows, :].astype(ref.dtype)


def ffn_kernel(count, members, *refs):
    chunks, blocks = refs[:count], refs[count : count + members]
    wg, wu, wd, nm, gate, up, hidden, keep, give = refs[count + members :]
    pc = wg.shape[0] // count
    rows = blocks[0].shape[0]
    for i in range(count):
        wg[i * pc : (i + 1) * pc, :] = chunks[i][:pc, :]
        wu[i * pc : (i + 1) * pc, :] = chunks[i][pc : 2 * pc, :]
        wd[i * pc : (i + 1) * pc, :] = chunks[i][2 * pc :, :]
    for i in range(members):
        nm[i * rows : (i + 1) * rows, :] = blocks[i][...]
    g = times_t(nm[...], wg[...])
    u = times_t(nm[...], wu[...])
    gate[...] = g
    up[...] = u
    t = jnp.tanh(root * (g + cubic * (g * g * g)))
    hid = (0.5 * g * (1.0 + t) * u).astype(bf)
    hidden[...] = hid
    split(times(hid, wd[...]), members, keep, give)


def ffn_end_kernel(keep, gave, resid, cot, gains, *refs):
    far, (out, d_ffn, dg) = refs[:-3], refs[-3:]
    rows = resid.shape[0]
    total = keep[:rows, :] + gave[:rows, :].astype(f32)
    for ref in far:
        total = total + ref[...].astype(f32)
    g = gains[3:4, :]
    out[...] = (resid[...] + norm(total, g)).astype(bf)
    d, dg[...] = norm_back(total, g, cot[...].astype(f32))
    d_ffn[...] = d.astype(bf)


def ffn_back_kernel(members, wg, wu, wd, gate, up, *refs):
    blocks = refs[:members]
    dall, dgate, dup, keep, give = refs[members:]
    rows = blocks[0].shape[0]
    for i in range(members):
        dall[i * rows : (i + 1) * rows, :] = blocks[i][...]
    d_hidden = times_t(dall[...], wd[...])
    g, u = gate[...], up[...]
    t = jnp.tanh(root * (g + cubic * (g * g * g)))
    slope = 0.5 * (1.0 + t) + 0.5 * g * (1.0 - t * t) * (root * (1.0 + 3.0 * cubic * (g * g)))
    dg = (d_hidden * u * slope).astype(bf)
    du = (d_hidden * (0.5 * g * (1.0 + t))).astype(bf)
    dgate[...] = dg
    dup[...] = du
    split(times(dg, wg[...]) + times(du, wu[...]), members, keep, give)


def ffn_grad_kernel(count, nm, dall, dgate, dup, hidden, keep, give):
    pc = hidden.shape[1] // count
    for k, (a, b) in enumerate(((dgate, nm), (dup, nm), (hidden, dall))):
        grad = t_times(a[...], b[...])
        for i in range(count):
            at = (i // 2) * 3 * pc + k * pc
            ref = give if i % 2 else keep
            ref[at : at + pc, :] = grad[i * pc : (i + 1) * pc, :].astype(ref.dtype)


def attend_back_kernel(seqs, heads, scale, keep, gave, resid, proj, cot, gains, wo, *refs):
    far = refs[:-11]
    probs, kall, qrot, d_resid, d_proj, dqrot, kkeep, kgive, dg_pf, dg_pa, dkall = refs[-11:]
    rows = resid.shape[0]
    hd = kall.shape[1] // 2
    span = rows // seqs
    length = kall.shape[0] // seqs
    total = keep[:rows, :] + gave[:rows, :].astype(f32)
    for ref in far:
        total = total + ref[...].astype(f32)
    d, dg_pf[...] = norm_back(resid[...], gains[2:3, :], total)
    d = d + cot[...].astype(f32)
    d_resid[...] = d
    d, dg_pa[...] = norm_back(proj[...], gains[1:2, :], d)
    d = d.astype(bf)
    d_proj[...] = d
    d_att = times_t(d, wo[...]).astype(bf)
    for s in range(seqs):
        at = slice(s * span, (s + 1) * span)
        keys = kall[s * length : (s + 1) * length, :hd]
        values = kall[s * length : (s + 1) * length, hd:]
        p = probs[s * heads * span : (s + 1) * heads * span, :]
        da = jnp.concatenate([d_att[at, h * hd : (h + 1) * hd] for h in range(heads)], axis=0)
        dp = times_t(da, values)
        delta = jnp.sum(p * dp, axis=-1, keepdims=True)
        ds = (p * (dp - delta) * scale).astype(bf)
        dq = times(ds, keys)
        for h in range(heads):
            dqrot[at, h * hd : (h + 1) * hd] = dq[h * span : (h + 1) * span, :]
        dkall[:, :hd] = t_times(ds, stacked(qrot, at, heads, hd))
        dkall[:, hd:] = t_times(p.astype(bf), da)
        for i in range(length // span):
            ref = kgive if i % 2 else kkeep
            to = (i // 2) * rows + s * span
            ref[to : to + span, :] = dkall[i * span : (i + 1) * span, :].astype(ref.dtype)


def unturn(d, c, s):
    half = d.shape[1] // 2
    a, b = d[:, :half], d[:, half:]
    return jnp.concatenate([a * c + b * s, b * c - a * s], axis=1)


def packed(count, where, sources, keep, give, tail=None):
    twin = where[count]
    sizes = [src.shape[0] // count // 2 for src in sources]
    each = sum(sizes)
    for i in range(count):
        block = where[i]
        to = ((i % 2) * (count // 2) + i // 2) * each
        for src, size in zip(sources, sizes):
            own = pl.multiple_of(block * (2 * size) + twin * size, 8)
            their = pl.multiple_of(block * (2 * size) + (1 - twin) * size, 8)
            keep[to : to + size, :] = src[pl.ds(own, size), :].astype(keep.dtype)
            give[to : to + size, :] = src[pl.ds(their, size), :].astype(bf)
            to += size
    if tail is not None:
        keep[count * each :, :] = tail.astype(keep.dtype)
        give[count * each :, :] = tail.astype(bf)


def query_back_kernel(
    count, heads, where, dqrot, qraw, gains, cosine, sine, nin, att, d_proj, dq, dg_q, keep, give, gq, go
):
    hd = qraw.shape[1] // heads
    c, s = cosine[...], sine[...]
    total = jnp.zeros((1, hd), f32)
    for h in range(heads):
        at = slice(h * hd, (h + 1) * hd)
        d, dg = norm_back(qraw[:, at], gains[4:5, :hd], unturn(dqrot[:, at], c, s))
        dq[:, at] = d.astype(bf)
        total = total + dg
    dg_q[...] = total
    gq[...] = t_times(dq[...], nin[...])
    go[...] = t_times(att[...], d_proj[...])
    packed(count, where, (gq, go), keep, give)


def key_back_kernel(
    count, where, kkeep, kgave, kraw, gains, cosine, sine, nin, dq, wq, wk, wv, x, d_resid, dg_po, dg_pf, dg_pa, dg_q, *refs
):
    far, (grad, keep, give, gk, gv) = refs[:-5], refs[-5:]
    rows, hd = kraw.shape
    total = kkeep[:rows, :] + kgave[:rows, :].astype(f32)
    for ref in far:
        total = total + ref[...].astype(f32)
    d, dg_k = norm_back(
        kraw[...], gains[5:6, :hd], unturn(total[:, :hd], cosine[...], sine[...])
    )
    dk = d.astype(bf)
    dv = total[:, hd:].astype(bf)
    d_in = times(dq[...], wq[...]) + times(dk, wk[...]) + times(dv, wv[...])
    d, dg_in = norm_back(x[...].astype(f32), gains[0:1, :], d_in)
    grad[...] = d_resid[...] + d
    gk[...] = t_times(dk, nin[...])
    gv[...] = t_times(dv, nin[...])
    pad = jnp.zeros((1, nin.shape[1] - hd), f32)
    none = jnp.zeros((2, nin.shape[1]), f32)
    tail = jnp.concatenate(
        [
            dg_in,
            dg_pa[...],
            dg_pf[...],
            dg_po[...],
            jnp.concatenate([dg_q[...], pad], axis=1),
            jnp.concatenate([dg_k, pad], axis=1),
            none,
        ],
        axis=0,
    )
    packed(count, where, (gk, gv), keep, give, tail)


def near_kernel(half, keep, gave, keep2, give2):
    tail = keep.shape[0] - 2 * half
    keep2[:half, :] = keep[:half, :].astype(f32) + gave[:half, :].astype(f32)
    rest = slice(half, 2 * half)
    give2[:half, :] = (keep[rest, :].astype(f32) + gave[rest, :].astype(f32)).astype(bf)
    if tail:
        t = keep[2 * half :, :].astype(f32) + gave[2 * half :, :].astype(f32)
        keep2[half:, :] = t
        give2[half:, :] = t.astype(bf)


def far_kernel(parts, rows, keep, gave, *outs):
    tail = keep.shape[0] - parts * rows
    for a in range(parts):
        at = slice(a * rows, (a + 1) * rows)
        outs[a][:rows, :] = (keep[at, :].astype(f32) + gave[at, :].astype(f32)).astype(outs[a].dtype)
    if tail:
        at = slice(parts * rows, parts * rows + tail)
        t = keep[at, :].astype(f32) + gave[at, :].astype(f32)
        for a in range(parts):
            outs[a][rows:, :] = t.astype(outs[a].dtype)


def ffn_out_kernel(members, where, *refs):
    blocks, (gate, up, down, buf) = refs[:members], refs[members:]
    pc = blocks[0].shape[0] // 3
    for k, out in enumerate((gate, up, down)):
        to_ref = out if k == 2 else buf
        for i in range(members):
            to = pl.multiple_of(where[i] * pc, 8)
            to_ref[pl.ds(to, pc), :] = blocks[i][k * pc : (k + 1) * pc, :].astype(f32)
        if k < 2:
            out[...] = buf[...].T


def joined(sizes, twin, mine, other, outs):
    def put(low, high):
        start = 0
        for size, out in zip(sizes, outs):
            half = size // 2
            rows = slice(start, start + half)
            start += half
            if out.shape[0] != size:
                out[...] = jnp.concatenate([low[rows, :], high[rows, :]], axis=0).astype(f32).T
            else:
                out[:half, :] = low[rows, :].astype(f32)
                out[half:, :] = high[rows, :].astype(f32)

    @pl.when(twin == 0)
    def _():
        put(mine, other)

    @pl.when(twin != 0)
    def _():
        put(other, mine)


def query_out_kernel(sizes, twin, mine, other, *outs):
    joined(sizes, twin[0], mine, other, outs)


def key_out_kernel(sizes, at, mine, other, out_k, out_v, *gains):
    joined(sizes, at[0], mine, other, (out_k, out_v))
    tail = mine[mine.shape[0] - 8 :, :]
    for first, last in ((0, 4), (4, 6)):
        size = gains[first].shape[0]
        shape = (tail.shape[1], size)
        row = lax.broadcasted_iota(jnp.int32, shape, 0)
        col = lax.broadcasted_iota(jnp.int32, shape, 1)
        own = times(tail, (row == at[1] * size + col).astype(f32).astype(bf))
        for i in range(first, last):
            gains[i][...] = own[i, :]


def shards(
    layer_input,
    out_cotangent,
    block_pairs,
    w_query,
    w_key,
    w_value,
    w_output,
    w_gate,
    w_up,
    w_down,
    input_gain,
    attnpost_gain,
    ffnpre_gain,
    ffnpost_gain,
    query_gain,
    key_gain,
):
    S, C = Axis("shard"), Axis("ctx")
    seqs, span, width = layer_input.shape
    rows = seqs * span
    members, count = C.size, S.size
    twin = C.rank % 2
    pq, pk, po, pf = w_query.shape[1], w_key.shape[1], w_output.shape[0], w_down.shape[0]
    hd = query_gain.shape[0] * count
    hq = pq * count
    heads = hq // hd
    scale = hd ** (-0.5)
    where = jnp.stack(S.sources() + [twin]).astype(jnp.int32)
    x = layer_input.reshape(rows, width)
    cot = out_cotangent.reshape(rows, width)

    small = [input_gain, attnpost_gain, ffnpre_gain, ffnpost_gain, query_gain, key_gain]

    def placed(same):
        size = same[0].shape[0]
        at = jnp.arange(width)[None, :] == S.rank * size + jnp.arange(size)[:, None]
        return times(jnp.stack(same), at.astype(bf)).astype(bf)

    gain_rows = jnp.concatenate([placed(small[:4]), placed(small[4:])], axis=0)
    gain_rows = jnp.pad(gain_rows, ((0, 8 - len(small)), (0, 0)))

    whole = jnp.concatenate([w_query.T, w_key.T, w_value.T], axis=0)
    piece = whole.shape[0] // 2
    own = jnp.where(twin == 0, whole[:piece], whole[piece:])
    first = jnp.concatenate([own, gain_rows], axis=0)
    mine = S.gather(first)
    other = [C.send(m, 0, 1) for m in mine]
    own = lax.dynamic_slice_in_dim(w_output, twin * (po // 2), po // 2, 0)
    mine_o = S.gather(after(own, *mine[2::2]))
    other_o = [C.send(m, 0, 1) for m in mine_o]

    pc = pf // members

    def part_of(w):
        return lax.dynamic_slice_in_dim(w, C.rank * pc, pc, 0)

    ffn = jnp.concatenate([part_of(w_gate.T), part_of(w_up.T), part_of(w_down)], axis=0)
    chunks = S.gather(after(ffn, *mine_o[2::2]))

    places = seq_positions(block_pairs, span // 2)
    kpos = jnp.concatenate(
        [lax.dynamic_index_in_dim(places, o, 1, keepdims=False) for o in C.sources()], axis=1
    )
    own_pos = lax.dynamic_index_in_dim(places, C.rank, 1, keepdims=False).reshape(rows)
    cosine, sine = rope_tables(own_pos, hd)
    qpos = own_pos[:, None]

    wq, wk, wv, gains, nin, qraw, kraw, qrot, kv = call(
        functools.partial(qkv_kernel, count, heads),
        [
            ((hq, width), bf),
            ((hd, width), bf),
            ((hd, width), bf),
            ((8, width), f32),
            ((rows, width), bf),
            ((rows, hq), f32),
            ((rows, hd), f32),
            ((rows, hq), bf),
            ((rows, 2 * hd), bf),
        ],
        (where, x, cosine, sine, *mine, *other),
        scalars=1,
    )
    kvs = C.gather(kv)
    length = members * span
    att, probs, kall, proj, resid, nmid, wo = call(
        functools.partial(attend_kernel, seqs, heads, scale, count),
        [
            ((rows, hq), bf),
            ((seqs * heads * span, length), f32),
            ((seqs * length, 2 * hd), bf),
            ((rows, width), f32),
            ((rows, width), f32),
            ((rows, width), bf),
            ((hq, width), bf),
        ],
        (where, qpos, kpos, qrot, x, gains, *mine_o, *other_o, *kvs),
        scalars=1,
    )
    hid = count * pc
    wg, wu, wd, nm, gate, up, hidden, keep, give = call(
        functools.partial(ffn_kernel, count, members),
        [
            ((hid, width), bf),
            ((hid, width), bf),
            ((hid, width), bf),
            ((members * rows, width), bf),
            ((members * rows, hid), f32),
            ((members * rows, hid), f32),
            ((members * rows, hid), bf),
            ((C.outer * rows, width), f32),
            ((C.outer * rows, width), bf),
        ],
        (*chunks, *C.gather(nmid)),
    )

    def home(keep, give):
        gave = C.send(give, 0, 1)
        far = []
        for a in range(1, C.outer):
            at = slice(a * rows, (a + 1) * rows)
            part = (keep[at] + gave[at].astype(f32)).astype(bf)
            far.append(C.send(part, C.outer - a, 0))
        return gave, far

    gave, far = home(keep, give)
    layer_output, d_ffn, dg_po = call(
        ffn_end_kernel,
        [((rows, width), bf), ((rows, width), bf), ((1, width), f32)],
        (keep, gave, resid, cot, gains, *far),
    )
    dall, dgate, dup, keep, give = call(
        functools.partial(ffn_back_kernel, members),
        [
            ((members * rows, width), bf),
            ((members * rows, hid), bf),
            ((members * rows, hid), bf),
            ((C.outer * rows, width), f32),
            ((C.outer * rows, width), bf),
        ],
        (wg, wu, wd, gate, up, *C.gather(d_ffn)),
    )
    gave, far = home(keep, give)

    def spread(keep, give, each):
        got = S.send(give, 0, 1)
        n = each + keep.shape[0] - S.outer * each
        parts = call(
            functools.partial(far_kernel, S.outer, each),
            [((n, width), f32)] + [((n, width), bf)] * (S.outer - 1),
            (keep, got),
        )
        return [parts[0]] + [S.send(parts[a], S.outer - a, 0) for a in range(1, S.outer)]

    def summed(terms):
        total = terms[0].astype(f32)
        for term in terms[1:]:
            total = total + term.astype(f32)
        return total.astype(bf)

    fkeep, fgive = call(
        functools.partial(ffn_grad_kernel, count),
        [((S.outer * 3 * pc, width), bf), ((S.outer * 3 * pc, width), bf)],
        (nm, dall, dgate, dup, hidden),
    )
    f_terms = spread(fkeep, fgive, 3 * pc)

    d_resid, d_proj, dqrot, kkeep, kgive, dg_pf, dg_pa = call(
        functools.partial(attend_back_kernel, seqs, heads, scale),
        [
            ((rows, width), f32),
            ((rows, width), bf),
            ((rows, hq), f32),
            ((C.outer * rows, 2 * hd), f32),
            ((C.outer * rows, 2 * hd), bf),
            ((1, width), f32),
            ((1, width), f32),
        ],
        (keep, gave, resid, proj, cot, gains, wo, *far, probs, kall, qrot),
        scratch=[pltpu.VMEM((length, 2 * hd), f32)],
    )
    kgave, kfar = home(kkeep, kgive)

    def begin(keep, give, each):
        got = C.send(give, 0, 1)
        half = S.outer * each
        n = keep.shape[0] - half
        keep, give = call(
            functools.partial(near_kernel, half), [((n, width), f32), ((n, width), bf)], (keep, got)
        )
        return spread(keep, give, each)

    def finish(terms):
        part = summed(terms)
        far = [C.send(part, a, 0) for a in range(1, C.outer)]
        total = summed([part] + far)
        return total, C.send(total, 0, 1)

    each_q, each_k = (pq + po) // 2, pk
    dq, dg_q, keep, give = call(
        functools.partial(query_back_kernel, count, heads),
        [
            ((rows, hq), bf),
            ((1, hd), f32),
            ((count * each_q, width), bf),
            ((count * each_q, width), bf),
        ],
        (where, dqrot, qraw, gains, cosine, sine, nin, att, d_proj),
        scalars=1,
        scratch=[pltpu.VMEM((hq, width), f32), pltpu.VMEM((hq, width), f32)],
    )
    q_terms = begin(keep, give, each_q)
    input_grad, keep, give = call(
        functools.partial(key_back_kernel, count),
        [
            ((rows, width), f32),
            ((count * each_k + 8, width), f32),
            ((count * each_k + 8, width), bf),
        ],
        (
            where,
            kkeep,
            kgave,
            kraw,
            gains,
            cosine,
            sine,
            nin,
            dq,
            wq,
            wk,
            wv,
            x,
            d_resid,
            dg_po,
            dg_pf,
            dg_pa,
            dg_q,
            *kfar,
        ),
        scalars=1,
        scratch=[pltpu.VMEM((hd, width), f32), pltpu.VMEM((hd, width), f32)],
    )
    k_terms = begin(keep, give, each_k)
    total_q = finish(q_terms)
    total_k = finish(k_terms)

    out_gate, out_up, out_down = call(
        functools.partial(ffn_out_kernel, members),
        [((width, pf), f32), ((width, pf), f32), ((pf, width), f32)],
        (jnp.stack(C.sources()).astype(jnp.int32), *C.gather(summed(f_terms))),
        scalars=1,
        scratch=[pltpu.VMEM((pf, width), f32)],
    )
    is_twin = twin.astype(jnp.int32)[None]
    out_query, out_output = call(
        functools.partial(query_out_kernel, (pq, po)),
        [((width, pq), f32), ((po, width), f32)],
        (is_twin, *total_q),
        scalars=1,
    )
    out_key, out_value, *sums = call(
        functools.partial(key_out_kernel, (pk, pk)),
        [((pk, width), f32), ((pk, width), f32)] + [(g.shape, f32) for g in small],
        (jnp.stack([twin, S.rank]).astype(jnp.int32), *total_k),
        scalars=1,
    )
    out_key, out_value = out_key.T, out_value.T
    return (
        layer_output.reshape(seqs, span, width),
        input_grad.reshape(seqs, span, width),
        out_query,
        out_key,
        out_value,
        out_output,
        out_gate,
        out_up,
        out_down,
        *sums,
    )


def solution(mesh):
    lead2 = P("shard", "ctx", None)
    cols = P(None, "shard")
    lead = P("shard", None)
    gain = P("shard")
    return jax.shard_map(
        shards,
        mesh=mesh,
        in_specs=(lead2, lead2, lead, cols, cols, cols, lead, cols, cols, lead) + (gain,) * 6,
        out_specs=(lead2, lead2, cols, cols, cols, lead, cols, cols, lead) + (gain,) * 6,
        check_vma=False,
    )
```

profile of v0, /device:TPU:0, one launch (start us, length us, event | category | flops | bytes accessed | tf_op | source)
XLA Modules:
  0.0 231.2 jit_solution(2533904124133466023)
XLA Ops:
  5.1 2.6 %collective-permute-start.13 = (bf16[104,640]{1,0:T(8,128)(2,1)S(1)}, bf16[104,640]{1,0:T(8,128)(2,1)S(1)}, u32[]{:S(2)}, u32[]{:S(2)}) collective-permute-start(bf16[104,640]{1,0:T(8,128)(2,1)S(1)} %pad_maximum_fusion.1.refs_0_), channel_id=1, source_target_pairs={{0,4},{4,0},{8,12},{12,8},{16,20},{20,16},{24,28},{28,24},{1,5},{5... | collective-permute-start | bytes 399368 | tf_op jit(solution)/shard_map/ppermute | solution.py:33
  7.7 3.6 %collective-permute-start.2 = (bf16[104,640]{1,0:T(8,128)(2,1)S(1)}, bf16[104,640]{1,0:T(8,128)(2,1)S(1)}, u32[]{:S(2)}, u32[]{:S(2)}) collective-permute-start(bf16[104,640]{1,0:T(8,128)(2,1)S(1)} %pad_maximum_fusion.1.refs_0_), channel_id=1, source_target_pairs={{0,24},{4,28},{8,0},{12,4},{16,8},{20,12},{24,16},{28,20},{1,25},{... | collective-permute-start | bytes 399368 | tf_op jit(solution)/shard_map/ppermute | solution.py:33
  15.3 7.8 %collective-permute-done.1.refs_4_ = bf16[104,640]{1,0:T(8,128)(2,1)S(1)} collective-permute-done((bf16[104,640]{1,0:T(8,128)(2,1)S(1)}, bf16[104,640]{1,0:T(8,128)(2,1)S(1)}, u32[]{:S(2)}, u32[]{:S(2)}) %collective-permute-start.1) | collective-permute-done | bytes 133152 | tf_op jit(solution)/shard_map/ppermute | solution.py:33
  30.5 3.7 %collective-permute-done.4.refs_4_ = bf16[64,640]{1,0:T(8,128)(2,1)S(1)} collective-permute-done((bf16[64,640]{1,0:T(8,128)(2,1)S(1)}, bf16[64,640]{1,0:T(8,128)(2,1)S(1)}, u32[]{:S(2)}, u32[]{:S(2)}) %collective-permute-start.4) | collective-permute-done | bytes 81952 | tf_op jit(solution)/shard_map/ppermute | solution.py:33
  47.6 3.6 %shard_map.271 = (bf16[1024,640]{1,0:T(8,128)(2,1)}, bf16[256,640]{1,0:T(8,128)(2,1)}, bf16[256,640]{1,0:T(8,128)(2,1)}, f32[8,640]{1,0:T(8,128)}, bf16[128,640]...) custom-call(s32[9]{0:T(128)} %stack.93.where, ...), custom_call_target="tpu_custom_call" | custom-call | tf_op jit(solution)/shard_map/pallas_call | solution.py:83
  63.1 4.7 %shard_map.272 = (bf16[128,1024]{1,0:T(8,128)(2,1)}, f32[512,256]{1,0:T(8,128)}, bf16[512,512]{1,0:T(8,128)(2,1)}, f32[128,640]{1,0:T(8,128)}, f32[128,640]{1,0:...) custom-call(s32[9]{0:T(128)} %stack.93.where, s32[128,1]{1,0:T(8,128)} %broadcast_in_dim_reshape.4.qpos, ...), custom_call_target="tpu_custom_call" | custom-call | tf_op jit(solution)/shard_map/pallas_call | solution.py:83
  69.9 8.2 %collective-permute-done.9.refs_4_ = bf16[192,640]{1,0:T(8,128)(2,1)S(1)} collective-permute-done((bf16[192,640]{1,0:T(8,128)(2,1)S(1)}, bf16[192,640]{1,0:T(8,128)(2,1)S(1)}, u32[]{:S(2)}, u32[]{:S(2)}) %collective-permute-start.9) | collective-permute-done | bytes 245792 | tf_op jit(solution)/shard_map/ppermute | solution.py:33
  80.7 6.3 %collective-permute-done.10.refs_5_ = bf16[192,640]{1,0:T(8,128)(2,1)S(1)} collective-permute-done((bf16[192,640]{1,0:T(8,128)(2,1)S(1)}, bf16[192,640]{1,0:T(8,128)(2,1)S(1)}, u32[]{:S(2)}, u32[]{:S(2)}) %collective-permute-start.10) | collective-permute-done | bytes 245792 | tf_op jit(solution)/shard_map/ppermute | solution.py:33
  87.0 3.6 %collective-permute-done.8.refs_3_ = bf16[192,640]{1,0:T(8,128)(2,1)S(1)} collective-permute-done((bf16[192,640]{1,0:T(8,128)(2,1)S(1)}, bf16[192,640]{1,0:T(8,128)(2,1)S(1)}, u32[]{:S(2)}, u32[]{:S(2)}) %collective-permute-start.8) | collective-permute-done | bytes 245792 | tf_op jit(solution)/shard_map/ppermute | solution.py:33
  92.0 5.0 %shard_map.273 = (bf16[512,640]{1,0:T(8,128)(2,1)}, bf16[512,640]{1,0:T(8,128)(2,1)}, bf16[512,640]{1,0:T(8,128)(2,1)}, bf16[512,640]{1,0:T(8,128)(2,1)}, f32[51...) custom-call(bf16[192,640]{1,0:T(8,128)(2,1)} %copy-done.4, ...), custom_call_target="tpu_custom_call" | custom-call | tf_op jit(solution)/shard_map/pallas_call | solution.py:83
  100.6 5.7 %collective-permute-done.44.refs_0_ = bf16[128,640]{1,0:T(8,128)(2,1)S(1)} collective-permute-done((bf16[128,640]{1,0:T(8,128)(2,1)S(1)}, bf16[128,640]{1,0:T(8,128)(2,1)S(1)}, u32[]{:S(2)}, u32[]{:S(2)}) %collective-permute-start.44) | collective-permute-done | bytes 163872 | tf_op jit(solution)/shard_map/ppermute | solution.py:33
  107.0 2.4 %shard_map.274 = (bf16[128,640]{1,0:T(8,128)(2,1)}, bf16[128,640]{1,0:T(8,128)(2,1)}, f32[1,640]{1,0:T(1,128)}) custom-call(f32[256,640]{1,0:T(8,128)} %get-tuple-element.101.keep, bf16[256,640]{1,0:T(8,128)(2,1)} %copy-done.6, f32[128,640]{1,0:T(8,128)} %get-tuple-element.103.resid, bf16[128,640]{1,0:T(8,128)(2,1)} %bitcast.47, ...), custom_call_target="tpu_custom_call" | custom-call | tf_op jit(solution)/shard_map/pallas_call | solution.py:83
  109.8 5.1 %collective-permute-done.46.refs_2_ = bf16[128,640]{1,0:T(8,128)(2,1)S(1)} collective-permute-done((bf16[128,640]{1,0:T(8,128)(2,1)}, bf16[128,640]{1,0:T(8,128)(2,1)S(1)}, u32[]{:S(2)}, u32[]{:S(2)}) %collective-permute-start.46) | collective-permute-done | bytes 163872 | tf_op jit(solution)/shard_map/ppermute | solution.py:33
  117.0 5.3 %shard_map.275 = (bf16[512,640]{1,0:T(8,128)(2,1)}, bf16[512,512]{1,0:T(8,128)(2,1)}, bf16[512,512]{1,0:T(8,128)(2,1)}, f32[256,640]{1,0:T(8,128)}, bf16[256,640]{1,0:T(8,128)(2,1)}) custom-call(bf16[512,640]{1,0:T(8,128)(2,1)} %get-tuple-element.105.wg, bf16[512,640]{1,0:T(8,128)(2,1)} %get-tuple-element.106.wu, bf16[512,640]{1,0:T(8,128)(2,1)} %get-tuple-element.107.wd, ...), custom_call_target="tpu_custom_call" | custom-call | tf_op jit(solution)/shard_map/pallas_call | solution.py:83
  125.8 5.7 %collective-permute-done.49.refs_0_ = bf16[128,640]{1,0:T(8,128)(2,1)S(1)} collective-permute-done((bf16[128,640]{1,0:T(8,128)(2,1)S(1)}, bf16[128,640]{1,0:T(8,128)(2,1)S(1)}, u32[]{:S(2)}, u32[]{:S(2)}) %collective-permute-start.49) | collective-permute-done | bytes 163872 | tf_op jit(solution)/shard_map/ppermute | solution.py:33
  132.2 4.8 %shard_map.276 = (f32[128,640]{1,0:T(8,128)}, bf16[128,640]{1,0:T(8,128)(2,1)}, f32[128,1024]{1,0:T(8,128)}, f32[256,512]{1,0:T(8,128)}, bf16[256,512]{1,0:T(8,1...) custom-call(f32[256,640]{1,0:T(8,128)} %get-tuple-element.111.keep, bf16[256,640]{1,0:T(8,128)(2,1)} %copy-done.7, ...), custom_call_target="tpu_custom_call" | custom-call | tf_op jit(solution)/shard_map/pallas_call | solution.py:83
  137.1 4.3 %shard_map.277 = (bf16[128,1024]{1,0:T(8,128)(2,1)}, f32[1,256]{1,0:T(1,128)}, bf16[1024,640]{1,0:T(8,128)(2,1)}, bf16[1024,640]{1,0:T(8,128)(2,1)}) custom-call(s32[9]{0:T(128)} %stack.93.where, f32[128,1024]{1,0:T(8,128)} %get-tuple-element.121.dqrot, f32[128,1024]{1,0:T(8,128)} %get-tuple-element.122.qraw, f32[8,640]{1,0:T(8,128)} %get-tuple-element.98.gains, ...), custom_call_target="tpu_custom_call" | custom-call | tf_op jit(solution)/shard_map/pallas_call | solution.py:83
  141.4 4.4 %shard_map.285 = (bf16[768,640]{1,0:T(8,128)(2,1)}, bf16[768,640]{1,0:T(8,128)(2,1)}) custom-call(bf16[512,640]{1,0:T(8,128)(2,1)} %get-tuple-element.155.nm, bf16[512,640]{1,0:T(8,128)(2,1)} %get-tuple-element.156.dall, bf16[512,512]{1,0:T(8,128)(2,1)} %get-tuple-element.157.dgate, bf16[512,512]{1,0:T(8,128)(2,1)} %get-tuple-element.158.dup, ...), custom_call_target="tpu_custom_call" | custom-call | tf_op jit(solution)/shard_map/pallas_call | solution.py:83
  148.7 3.2 %shard_map.279 = (f32[512,640]{1,0:T(8,128)}, bf16[512,640]{1,0:T(8,128)(2,1)}) custom-call(bf16[1024,640]{1,0:T(8,128)(2,1)} %get-tuple-element.135.keep, bf16[1024,640]{1,0:T(8,128)(2,1)} %copy-done.1), custom_call_target="tpu_custom_call" | custom-call | tf_op jit(solution)/shard_map/pallas_call | solution.py:83
  153.0 4.9 %collective-permute-done.51.refs_0_ = bf16[128,512]{1,0:T(8,128)(2,1)S(1)} collective-permute-done((bf16[128,512]{1,0:T(8,128)(2,1)S(1)}, bf16[128,512]{1,0:T(8,128)(2,1)S(1)}, u32[]{:S(2)}, u32[]{:S(2)}) %collective-permute-start.51) | collective-permute-done | bytes 131104 | tf_op jit(solution)/shard_map/ppermute | solution.py:33
  158.6 3.9 %shard_map.278 = (f32[128,640]{1,0:T(8,128)}, f32[264,640]{1,0:T(8,128)}, bf16[264,640]{1,0:T(8,128)(2,1)}) custom-call(s32[9]{0:T(128)} %stack.93.where, f32[256,512]{1,0:T(8,128)} %get-tuple-element.117.kkeep, bf16[256,512]{1,0:T(8,128)(2,1)} %copy-done.10, f32[128,256]{1,0:T(8,128)} %get-tuple-element.119.kraw, f32[8,640]{1,0:T(8,128)} %get-tuple-element.98.gains, ...), custom_call_target="tpu_custom_call" | custom-call | tf_op jit(solution)/shard_map/pallas_call | solution.py:83
  162.5 8.2 %collective-permute-done.66.gave = bf16[768,640]{1,0:T(8,128)(2,1)S(1)} collective-permute-done((bf16[768,640]{1,0:T(8,128)(2,1)}, bf16[768,640]{1,0:T(8,128)(2,1)S(1)}, u32[]{:S(2)}, u32[]{:S(2)}) %collective-permute-start.66) | collective-permute-done | bytes 983072 | tf_op jit(solution)/shard_map/ppermute | solution.py:33
  171.7 2.6 %shard_map.286 = (f32[192,640]{1,0:T(8,128)}, bf16[192,640]{1,0:T(8,128)(2,1)}, bf16[192,640]{1,0:T(8,128)(2,1)}, bf16[192,640]{1,0:T(8,128)(2,1)}) custom-call(bf16[768,640]{1,0:T(8,128)(2,1)} %get-tuple-element.160.keep, bf16[768,640]{1,0:T(8,128)(2,1)} %copy-done.3), custom_call_target="tpu_custom_call" | custom-call | tf_op jit(solution)/shard_map/pallas_call | solution.py:83
  174.3 2.0 collective-permute-start.69
  177.7 2.1 shard_map.282
  181.3 3.5 %collective-permute-done.53.gave = bf16[512,640]{1,0:T(8,128)(2,1)S(1)} collective-permute-done((bf16[512,640]{1,0:T(8,128)(2,1)}, bf16[512,640]{1,0:T(8,128)(2,1)S(1)}, u32[]{:S(2)}, u32[]{:S(2)}) %collective-permute-start.53) | collective-permute-done | bytes 655392 | tf_op jit(solution)/shard_map/ppermute | solution.py:33
  185.6 2.4 %shard_map.280 = (f32[128,640]{1,0:T(8,128)}, bf16[128,640]{1,0:T(8,128)(2,1)}, bf16[128,640]{1,0:T(8,128)(2,1)}, bf16[128,640]{1,0:T(8,128)(2,1)}) custom-call(f32[512,640]{1,0:T(8,128)} %get-tuple-element.137.keep, bf16[512,640]{1,0:T(8,128)(2,1)} %copy-done.9), custom_call_target="tpu_custom_call" | custom-call | tf_op jit(solution)/shard_map/pallas_call | solution.py:83
  189.5 12.6 %collective-permute-done.68 = bf16[192,640]{1,0:T(8,128)(2,1)S(1)} collective-permute-done((bf16[192,640]{1,0:T(8,128)(2,1)}, bf16[192,640]{1,0:T(8,128)(2,1)S(1)}, u32[]{:S(2)}, u32[]{:S(2)}) %collective-permute-start.68) | collective-permute-done | bytes 245792 | tf_op jit(solution)/shard_map/ppermute | solution.py:33
  205.6 3.8 %collective-permute-start.61 = (bf16[40,640]{1,0:T(8,128)(2,1)}, bf16[40,640]{1,0:T(8,128)(2,1)S(1)}, u32[]{:S(2)}, u32[]{:S(2)}) collective-permute-start(bf16[40,640]{1,0:T(8,128)(2,1)} %get-tuple-element.149), channel_id=1, source_target_pairs={{0,24},{4,28},{8,0},{12,4},{16,8},{20,12},{24,16},{28,20},{1,25},{... | collective-permute-start | bytes 153608 | tf_op jit(solution)/shard_map/ppermute | solution.py:33
  218.4 2.4 %collective-permute-done.64 = bf16[40,640]{1,0:T(8,128)(2,1)S(1)} collective-permute-done((bf16[40,640]{1,0:T(8,128)(2,1)S(1)}, bf16[40,640]{1,0:T(8,128)(2,1)S(1)}, u32[]{:S(2)}, u32[]{:S(2)}) %collective-permute-start.64) | collective-permute-done | bytes 51232 | tf_op jit(solution)/shard_map/ppermute | solution.py:33
  225.7 2.9 %shard_map.287 = (f32[640,256]{1,0:T(8,128)}, f32[640,256]{1,0:T(8,128)}, f32[256,640]{1,0:T(8,128)}) custom-call(s32[4]{0:T(128)} %pad_add_fusion.2.where, bf16[192,640]{1,0:T(8,128)(2,1)} %copy-done.5, bf16[192,640]{1,0:T(8,128)(2,1)} %copy-done.19, bf16[192,640]{1,0:T(8,128)(2,1)} %copy-done.17, bf16[192,640]{1,0:T(8,128)(2,1)} %copy-done.24), custom_call_target="tpu_custom_call" | custom-call | tf_op jit(solution)/shard_map/pallas_call | solution.py:83
  229.3 2.0 shard_map.281
  (306 shorter events, 86.5 us)
Async XLA Ops:
  4.5 20.6 %collective-permute-start.17 = (bf16[104,640]{1,0:T(8,128)(2,1)S(1)}, bf16[104,640]{1,0:T(8,128)(2,1)S(1)}, u32[]{:S(2)}, u32[]{:S(2)}) collective-permute-start(bf16[104,640]{1,0:T(8,128)(2,1)S(1)} %pad_maximum_fusion.1.refs_0_), channel_id=1, source_target_pairs={{0,1},{1,0},{2,3},{3,2},{4,5},{5,4},{6,7},{7,6},{8,9},{9,8},{10,11... | collective-permute-start | bytes 399368 | tf_op jit(solution)/shard_map/ppermute | solution.py:33
  5.1 21.1 %collective-permute-start.13 = (bf16[104,640]{1,0:T(8,128)(2,1)S(1)}, bf16[104,640]{1,0:T(8,128)(2,1)S(1)}, u32[]{:S(2)}, u32[]{:S(2)}) collective-permute-start(bf16[104,640]{1,0:T(8,128)(2,1)S(1)} %pad_maximum_fusion.1.refs_0_), channel_id=1, source_target_pairs={{0,4},{4,0},{8,12},{12,8},{16,20},{20,16},{24,28},{28,24},{1,5},{5... | collective-permute-start | bytes 399368 | tf_op jit(solution)/shard_map/ppermute | solution.py:33
  11.3 11.8 %collective-permute-start.1 = (bf16[104,640]{1,0:T(8,128)(2,1)S(1)}, bf16[104,640]{1,0:T(8,128)(2,1)S(1)}, u32[]{:S(2)}, u32[]{:S(2)}) collective-permute-start(bf16[104,640]{1,0:T(8,128)(2,1)S(1)} %pad_maximum_fusion.1.refs_0_), channel_id=1, source_target_pairs={{0,16},{4,20},{8,24},{12,28},{16,0},{20,4},{24,8},{28,12},{1,17},{... | collective-permute-start | bytes 399368 | tf_op jit(solution)/shard_map/ppermute | solution.py:33
  11.3 11.8 %collective-permute-start = (bf16[104,640]{1,0:T(8,128)(2,1)S(1)}, bf16[104,640]{1,0:T(8,128)(2,1)S(1)}, u32[]{:S(2)}, u32[]{:S(2)}) collective-permute-start(bf16[104,640]{1,0:T(8,128)(2,1)S(1)} %pad_maximum_fusion.1.refs_0_), channel_id=1, source_target_pairs={{0,8},{4,12},{8,16},{12,20},{16,24},{20,28},{24,0},{28,4},{1,9},{5... | collective-permute-start | bytes 399368 | tf_op jit(solution)/shard_map/ppermute | solution.py:33
  25.2 9.1 %collective-permute-start.4 = (bf16[64,640]{1,0:T(8,128)(2,1)S(1)}, bf16[64,640]{1,0:T(8,128)(2,1)S(1)}, u32[]{:S(2)}, u32[]{:S(2)}) collective-permute-start(bf16[64,640]{1,0:T(8,128)(2,1)S(1)} %constant_dynamic-slice_fusion.5.refs_0_), channel_id=1, source_target_pairs={{0,16},{4,20},{8,24},{12,28},{16,0},{20,4},{24,8},{28,12},{1,17},{... | collective-permute-start | bytes 245768 | tf_op jit(solution)/shard_map/ppermute | solution.py:33
  26.2 9.5 %collective-permute-start.3 = (bf16[64,640]{1,0:T(8,128)(2,1)S(1)}, bf16[64,640]{1,0:T(8,128)(2,1)S(1)}, u32[]{:S(2)}, u32[]{:S(2)}) collective-permute-start(bf16[64,640]{1,0:T(8,128)(2,1)S(1)} %constant_dynamic-slice_fusion.5.refs_0_), channel_id=1, source_target_pairs={{0,8},{4,12},{8,16},{12,20},{16,24},{20,28},{24,0},{28,4},{1,9},{5... | collective-permute-start | bytes 245768 | tf_op jit(solution)/shard_map/ppermute | solution.py:33
  28.3 8.9 %collective-permute-start.23 = (bf16[104,640]{1,0:T(8,128)(2,1)S(1)}, bf16[104,640]{1,0:T(8,128)(2,1)S(1)}, u32[]{:S(2)}, u32[]{:S(2)}) collective-permute-start(bf16[104,640]{1,0:T(8,128)(2,1)S(1)} %collective-permute-done.2.refs_6_), channel_id=1, source_target_pairs={{0,1},{1,0},{2,3},{3,2},{4,5},{5,4},{6,7},{7,6},{8,9},{9,8},{10,11... | collective-permute-start | bytes 399368 | tf_op jit(solution)/shard_map/ppermute | solution.py:33
  28.4 9.2 %collective-permute-start.16 = (bf16[104,640]{1,0:T(8,128)(2,1)S(1)}, bf16[104,640]{1,0:T(8,128)(2,1)S(1)}, u32[]{:S(2)}, u32[]{:S(2)}) collective-permute-start(bf16[104,640]{1,0:T(8,128)(2,1)S(1)} %collective-permute-done.2.refs_6_), channel_id=1, source_target_pairs={{0,4},{4,0},{8,12},{12,8},{16,20},{20,16},{24,28},{28,24},{1,5},{5... | collective-permute-start | bytes 399368 | tf_op jit(solution)/shard_map/ppermute | solution.py:33
  37.8 8.1 %collective-permute-start.22 = (bf16[104,640]{1,0:T(8,128)(2,1)S(1)}, bf16[104,640]{1,0:T(8,128)(2,1)S(1)}, u32[]{:S(2)}, u32[]{:S(2)}) collective-permute-start(bf16[104,640]{1,0:T(8,128)(2,1)S(1)} %collective-permute-done.15.refs_5_), channel_id=1, source_target_pairs={{0,1},{1,0},{2,3},{3,2},{4,5},{5,4},{6,7},{7,6},{8,9},{9,8},{10,11... | collective-permute-start | bytes 399368 | tf_op jit(solution)/shard_map/ppermute | solution.py:33
  45.9 7.8 %collective-permute-start.31 = (bf16[64,640]{1,0:T(8,128)(2,1)S(1)}, bf16[64,640]{1,0:T(8,128)(2,1)S(1)}, u32[]{:S(2)}, u32[]{:S(2)}) collective-permute-start(bf16[64,640]{1,0:T(8,128)(2,1)S(1)} %collective-permute-done.3.refs_2_), channel_id=1, source_target_pairs={{0,1},{1,0},{2,3},{3,2},{4,5},{5,4},{6,7},{7,6},{8,9},{9,8},{10,11... | collective-permute-start | bytes 245768 | tf_op jit(solution)/shard_map/ppermute | solution.py:33
  54.4 15.0 %collective-permute-start.11 = (bf16[192,640]{1,0:T(8,128)(2,1)S(1)}, bf16[192,640]{1,0:T(8,128)(2,1)S(1)}, u32[]{:S(2)}, u32[]{:S(2)}) collective-permute-start(bf16[192,640]{1,0:T(8,128)(2,1)S(1)} %pad_maximum_fusion.refs_0_), channel_id=1, source_target_pairs={{0,24},{4,28},{8,0},{12,4},{16,8},{20,12},{24,16},{28,20},{1,25},{... | collective-permute-start | bytes 737288 | tf_op jit(solution)/shard_map/ppermute | solution.py:33
  56.3 21.9 %collective-permute-start.9 = (bf16[192,640]{1,0:T(8,128)(2,1)S(1)}, bf16[192,640]{1,0:T(8,128)(2,1)S(1)}, u32[]{:S(2)}, u32[]{:S(2)}) collective-permute-start(bf16[192,640]{1,0:T(8,128)(2,1)S(1)} %pad_maximum_fusion.refs_0_), channel_id=1, source_target_pairs={{0,16},{4,20},{8,24},{12,28},{16,0},{20,4},{24,8},{28,12},{1,17},{... | collective-permute-start | bytes 737288 | tf_op jit(solution)/shard_map/ppermute | solution.py:33
  56.4 23.3 %collective-permute-start.7 = (bf16[192,640]{1,0:T(8,128)(2,1)S(1)}, bf16[192,640]{1,0:T(8,128)(2,1)S(1)}, u32[]{:S(2)}, u32[]{:S(2)}) collective-permute-start(bf16[192,640]{1,0:T(8,128)(2,1)S(1)} %pad_maximum_fusion.refs_0_), channel_id=1, source_target_pairs={{0,8},{4,12},{8,16},{12,20},{16,24},{20,28},{24,0},{28,4},{1,9},{5... | collective-permute-start | bytes 737288 | tf_op jit(solution)/shard_map/ppermute | solution.py:33
  59.6 20.6 %collective-permute-start.6 = (bf16[192,640]{1,0:T(8,128)(2,1)S(1)}, bf16[192,640]{1,0:T(8,128)(2,1)S(1)}, u32[]{:S(2)}, u32[]{:S(2)}) collective-permute-start(bf16[192,640]{1,0:T(8,128)(2,1)S(1)} %pad_maximum_fusion.refs_0_), channel_id=1, source_target_pairs={{0,4},{4,0},{8,12},{12,8},{16,20},{20,16},{24,28},{28,24},{1,5},{5... | collective-permute-start | bytes 737288 | tf_op jit(solution)/shard_map/ppermute | solution.py:33
  67.8 12.4 %collective-permute-start.41 = (bf16[128,640]{1,0:T(8,128)(2,1)}, bf16[128,640]{1,0:T(8,128)(2,1)S(1)}, u32[]{:S(2)}, u32[]{:S(2)}) collective-permute-start(bf16[128,640]{1,0:T(8,128)(2,1)} %get-tuple-element.100.refs_8_), channel_id=1, source_target_pairs={{0,2},{1,3},{2,0},{3,1},{4,6},{5,7},{6,4},{7,5},{8,10},{9,11},{10,... | collective-permute-start | bytes 491528 | tf_op jit(solution)/shard_map/ppermute | solution.py:33
  69.4 11.3 %collective-permute-start.12 = (bf16[192,640]{1,0:T(8,128)(2,1)S(1)}, bf16[192,640]{1,0:T(8,128)(2,1)S(1)}, u32[]{:S(2)}, u32[]{:S(2)}) collective-permute-start(bf16[192,640]{1,0:T(8,128)(2,1)S(1)} %collective-permute-done.11.refs_6_), channel_id=1, source_target_pairs={{0,4},{4,0},{8,12},{12,8},{16,20},{20,16},{24,28},{28,24},{1,5},{5... | collective-permute-start | bytes 737288 | tf_op jit(solution)/shard_map/ppermute | solution.py:33
  78.2 8.8 %collective-permute-start.10 = (bf16[192,640]{1,0:T(8,128)(2,1)S(1)}, bf16[192,640]{1,0:T(8,128)(2,1)S(1)}, u32[]{:S(2)}, u32[]{:S(2)}) collective-permute-start(bf16[192,640]{1,0:T(8,128)(2,1)S(1)} %collective-permute-done.9.refs_4_), channel_id=1, source_target_pairs={{0,4},{4,0},{8,12},{12,8},{16,20},{20,16},{24,28},{28,24},{1,5},{5... | collective-permute-start | bytes 737288 | tf_op jit(solution)/shard_map/ppermute | solution.py:33
  79.7 10.9 %collective-permute-start.8 = (bf16[192,640]{1,0:T(8,128)(2,1)S(1)}, bf16[192,640]{1,0:T(8,128)(2,1)S(1)}, u32[]{:S(2)}, u32[]{:S(2)}) collective-permute-start(bf16[192,640]{1,0:T(8,128)(2,1)S(1)} %collective-permute-done.7.refs_2_), channel_id=1, source_target_pairs={{0,4},{4,0},{8,12},{12,8},{16,20},{20,16},{24,28},{28,24},{1,5},{5... | collective-permute-start | bytes 737288 | tf_op jit(solution)/shard_map/ppermute | solution.py:33
  80.2 10.4 %collective-permute-start.40 = (bf16[128,640]{1,0:T(8,128)(2,1)}, bf16[128,640]{1,0:T(8,128)(2,1)S(1)}, u32[]{:S(2)}, u32[]{:S(2)}) collective-permute-start(bf16[128,640]{1,0:T(8,128)(2,1)} %get-tuple-element.100.refs_8_), channel_id=1, source_target_pairs={{0,1},{1,0},{2,3},{3,2},{4,5},{5,4},{6,7},{7,6},{8,9},{9,8},{10,11... | collective-permute-start | bytes 491528 | tf_op jit(solution)/shard_map/ppermute | solution.py:33
  80.2 10.4 %collective-permute-start.42 = (bf16[128,640]{1,0:T(8,128)(2,1)S(1)}, bf16[128,640]{1,0:T(8,128)(2,1)S(1)}, u32[]{:S(2)}, u32[]{:S(2)}) collective-permute-start(bf16[128,640]{1,0:T(8,128)(2,1)S(1)} %collective-permute-done.41.refs_10_), channel_id=1, source_target_pairs={{0,1},{1,0},{2,3},{3,2},{4,5},{5,4},{6,7},{7,6},{8,9},{9,8},{10,11... | collective-permute-start | bytes 491528 | tf_op jit(solution)/shard_map/ppermute | solution.py:33
  145.9 24.8 %collective-permute-start.66 = (bf16[768,640]{1,0:T(8,128)(2,1)}, bf16[768,640]{1,0:T(8,128)(2,1)S(1)}, u32[]{:S(2)}, u32[]{:S(2)}) collective-permute-start(bf16[768,640]{1,0:T(8,128)(2,1)} %get-tuple-element.161), channel_id=1, source_target_pairs={{0,4},{4,0},{8,12},{12,8},{16,20},{20,16},{24,28},{28,24},{1,5},{5... | collective-permute-start | bytes 2949128 | tf_op jit(solution)/shard_map/ppermute | solution.py:33
  151.9 32.9 %collective-permute-start.53 = (bf16[512,640]{1,0:T(8,128)(2,1)}, bf16[512,640]{1,0:T(8,128)(2,1)S(1)}, u32[]{:S(2)}, u32[]{:S(2)}) collective-permute-start(bf16[512,640]{1,0:T(8,128)(2,1)} %get-tuple-element.138), channel_id=1, source_target_pairs={{0,4},{4,0},{8,12},{12,8},{16,20},{20,16},{24,28},{28,24},{1,5},{5... | collective-permute-start | bytes 1966088 | tf_op jit(solution)/shard_map/ppermute | solution.py:33
  162.5 14.4 %collective-permute-start.59 = (bf16[264,640]{1,0:T(8,128)(2,1)}, bf16[264,640]{1,0:T(8,128)(2,1)S(1)}, u32[]{:S(2)}, u32[]{:S(2)}) collective-permute-start(bf16[264,640]{1,0:T(8,128)(2,1)} %get-tuple-element.145), channel_id=1, source_target_pairs={{0,1},{1,0},{2,3},{3,2},{4,5},{5,4},{6,7},{7,6},{8,9},{9,8},{10,11... | collective-permute-start | bytes 1013768 | tf_op jit(solution)/shard_map/ppermute | solution.py:33
  174.3 13.7 %collective-permute-start.67 = (bf16[192,640]{1,0:T(8,128)(2,1)}, bf16[192,640]{1,0:T(8,128)(2,1)S(1)}, u32[]{:S(2)}, u32[]{:S(2)}) collective-permute-start(bf16[192,640]{1,0:T(8,128)(2,1)} %get-tuple-element.163), channel_id=1, source_target_pairs={{0,24},{4,28},{8,0},{12,4},{16,8},{20,12},{24,16},{28,20},{1,25},{... | collective-permute-start | bytes 737288 | tf_op jit(solution)/shard_map/ppermute | solution.py:33
  174.3 27.9 %collective-permute-start.68 = (bf16[192,640]{1,0:T(8,128)(2,1)}, bf16[192,640]{1,0:T(8,128)(2,1)S(1)}, u32[]{:S(2)}, u32[]{:S(2)}) collective-permute-start(bf16[192,640]{1,0:T(8,128)(2,1)} %get-tuple-element.164), channel_id=1, source_target_pairs={{0,16},{4,20},{8,24},{12,28},{16,0},{20,4},{24,8},{28,12},{1,17},{... | collective-permute-start | bytes 737288 | tf_op jit(solution)/shard_map/ppermute | solution.py:33
  174.3 27.9 %collective-permute-start.69 = (bf16[192,640]{1,0:T(8,128)(2,1)}, bf16[192,640]{1,0:T(8,128)(2,1)S(1)}, u32[]{:S(2)}, u32[]{:S(2)}) collective-permute-start(bf16[192,640]{1,0:T(8,128)(2,1)} %get-tuple-element.165), channel_id=1, source_target_pairs={{0,8},{4,12},{8,16},{12,20},{16,24},{20,28},{24,0},{28,4},{1,9},{5... | collective-permute-start | bytes 737288 | tf_op jit(solution)/shard_map/ppermute | solution.py:33
  179.8 23.5 %collective-permute-start.60 = (bf16[136,640]{1,0:T(8,128)(2,1)}, bf16[136,640]{1,0:T(8,128)(2,1)S(1)}, u32[]{:S(2)}, u32[]{:S(2)}) collective-permute-start(bf16[136,640]{1,0:T(8,128)(2,1)} %get-tuple-element.147), channel_id=1, source_target_pairs={{0,4},{4,0},{8,12},{12,8},{16,20},{20,16},{24,28},{28,24},{1,5},{5... | collective-permute-start | bytes 522248 | tf_op jit(solution)/shard_map/ppermute | solution.py:33
  188.0 17.7 %collective-permute-start.54 = (bf16[128,640]{1,0:T(8,128)(2,1)}, bf16[128,640]{1,0:T(8,128)(2,1)S(1)}, u32[]{:S(2)}, u32[]{:S(2)}) collective-permute-start(bf16[128,640]{1,0:T(8,128)(2,1)} %get-tuple-element.140), channel_id=1, source_target_pairs={{0,24},{4,28},{8,0},{12,4},{16,8},{20,12},{24,16},{28,20},{1,25},{... | collective-permute-start | bytes 491528 | tf_op jit(solution)/shard_map/ppermute | solution.py:33
  188.0 21.5 %collective-permute-start.55 = (bf16[128,640]{1,0:T(8,128)(2,1)}, bf16[128,640]{1,0:T(8,128)(2,1)S(1)}, u32[]{:S(2)}, u32[]{:S(2)}) collective-permute-start(bf16[128,640]{1,0:T(8,128)(2,1)} %get-tuple-element.141), channel_id=1, source_target_pairs={{0,16},{4,20},{8,24},{12,28},{16,0},{20,4},{24,8},{28,12},{1,17},{... | collective-permute-start | bytes 491528 | tf_op jit(solution)/shard_map/ppermute | solution.py:33
  202.3 15.5 %collective-permute-start.71 = (bf16[192,640]{1,0:T(8,128)(2,1)S(1)}, bf16[192,640]{1,0:T(8,128)(2,1)S(1)}, u32[]{:S(2)}, u32[]{:S(2)}) collective-permute-start(bf16[192,640]{1,0:T(8,128)(2,1)S(1)} %add_convert_fusion.refs_0_), channel_id=1, source_target_pairs={{0,2},{1,3},{2,0},{3,1},{4,6},{5,7},{6,4},{7,5},{8,10},{9,11},{10,... | collective-permute-start | bytes 737288 | tf_op jit(solution)/shard_map/ppermute | solution.py:33
  203.2 21.1 %collective-permute-start.70 = (bf16[192,640]{1,0:T(8,128)(2,1)S(1)}, bf16[192,640]{1,0:T(8,128)(2,1)S(1)}, u32[]{:S(2)}, u32[]{:S(2)}) collective-permute-start(bf16[192,640]{1,0:T(8,128)(2,1)S(1)} %add_convert_fusion.refs_0_), channel_id=1, source_target_pairs={{0,1},{1,0},{2,3},{3,2},{4,5},{5,4},{6,7},{7,6},{8,9},{9,8},{10,11... | collective-permute-start | bytes 737288 | tf_op jit(solution)/shard_map/ppermute | solution.py:33
  217.9 10.7 %collective-permute-start.58 = (bf16[128,640]{1,0:T(8,128)(2,1)S(1)}, bf16[128,640]{1,0:T(8,128)(2,1)S(1)}, u32[]{:S(2)}, u32[]{:S(2)}) collective-permute-start(bf16[128,640]{1,0:T(8,128)(2,1)S(1)} %add_convert_fusion.1.mine), channel_id=1, source_target_pairs={{0,1},{1,0},{2,3},{3,2},{4,5},{5,4},{6,7},{7,6},{8,9},{9,8},{10,11... | collective-permute-start | bytes 491528 | tf_op jit(solution)/shard_map/ppermute | solution.py:33
  (110 other events, 989.4 us)
where the time goes:
time: 232 us; the launch traced here: 231 us
  waiting for transfers between devices  91.5 us (39%)
  Pallas kernels  56.8 us (24%)
  starting transfers between devices  52.6 us (23%)
  local copies, waits for them, and re-layouts  17.7 us (8%)
  other arithmetic  9.34 us (4%)
    ppermute x73, waiting for transfers between devices, send(): return lax.ppermute(x, self.name, pairs)  91.5 us
    pallas_call x17, Pallas kernels, call(): pl.pallas_call(body, out_shape=[jax.ShapeDtypeStruct(shape, kind) for sha...  56.8 us
    ppermute x73, starting transfers between devices, send(): return lax.ppermute(x, self.name, pairs)  52.6 us
    unnamed x142, local copies, waits for them, and re-layouts  14.4 us
  transfers between devices with their start and end apart: 73, of which 26 were waited for; matrix products, arithmetic and copies ran while one was open for 5% of the time, Pallas kernels for 14%

commit v1 on v0

--- a/solution.py
+++ b/solution.py
@@ -136,10 +136,10 @@
 
 def qkv_kernel(count, heads, where, x, cosine, sine, *refs):
     mine, other = refs[:count], refs[count : 2 * count]
-    wq, wk, wv, gains, nin, qraw, kraw, qrot, kv = refs[2 * count :]
-    piece = (wq.shape[0] + wk.shape[0] + wv.shape[0]) // count // 2
+    wq, wk, wv, wo, gains, nin, qraw, kraw, qrot, kv = refs[2 * count :]
+    piece = sum(w.shape[0] for w in (wq, wk, wv, wo)) // count // 2
     hd = wk.shape[0]
-    unpack(where, mine, other, piece, (wq, wk, wv))
+    unpack(where, mine, other, piece, (wq, wk, wv, wo))
     total = mine[0][piece:, :].astype(f32)
     for i in range(1, count):
         total = total + mine[i][piece:, :].astype(f32)
@@ -171,10 +171,9 @@
     return jnp.concatenate([ref[rows, h * hd : (h + 1) * hd] for h in range(heads)], axis=0)
 
 
-def attend_kernel(seqs, heads, scale, count, where, qpos, kpos, qrot, x, gains, *refs):
-    mine, other, blocks = refs[:count], refs[count : 2 * count], refs[2 * count : -7]
-    att, probs, kall, proj, resid, nmid, wo = refs[-7:]
-    unpack(where, mine, other, mine[0].shape[0], (wo,))
+def attend_kernel(seqs, heads, scale, qpos, kpos, qrot, x, wo, gains, *refs):
+    blocks = refs[:-6]
+    att, probs, kall, proj, resid, nmid = refs[-6:]
     hd = kall.shape[1] // 2
     span = qrot.shape[0] // seqs
     length = len(blocks) * span
@@ -393,6 +392,17 @@
         give2[half:, :] = t.astype(bf)
 
 
+def part_kernel(parts, blocks, outer, keep, gave, own, *gives):
+    rows = keep.shape[0] // blocks
+    size = rows // parts
+    for a, out in enumerate((own, *gives)):
+        part = lax.rem(outer[0] + a, parts)
+        for i in range(blocks):
+            at = pl.ds(pl.multiple_of(i * rows + part * size, 8), size)
+            total = keep[at, :].astype(f32) + gave[at, :].astype(f32)
+            out[i * size : (i + 1) * size, :] = total.astype(out.dtype)
+
+
 def far_kernel(parts, rows, keep, gave, *outs):
     tail = keep.shape[0] - parts * rows
     for a in range(parts):
@@ -424,11 +434,8 @@
             half = size // 2
             rows = slice(start, start + half)
             start += half
-            if out.shape[0] != size:
-                out[...] = jnp.concatenate([low[rows, :], high[rows, :]], axis=0).astype(f32).T
-            else:
-                out[:half, :] = low[rows, :].astype(f32)
-                out[half:, :] = high[rows, :].astype(f32)
+            out[:half, :] = low[rows, :].astype(f32)
+            out[half:, :] = high[rows, :].astype(f32)
 
     @pl.when(twin == 0)
     def _():
@@ -439,8 +446,17 @@
         put(other, mine)
 
 
-def query_out_kernel(sizes, twin, mine, other, *outs):
-    joined(sizes, twin[0], mine, other, outs)
+def query_out_kernel(sizes, where, *refs):
+    blocks, (out_q, out_o, buf) = refs[:-3], refs[-3:]
+    size = blocks[0].shape[0]
+    half = buf.shape[0] // 2
+    for i, block in enumerate(blocks):
+        to = pl.multiple_of(lax.rem(where[i], 2) * half + where[i] // 2 * size, 8)
+        buf[pl.ds(to, size), :] = block[...].astype(f32)
+    low, high = sizes[0] // 2, sizes[1] // 2
+    out_q[...] = jnp.concatenate([buf[:low, :], buf[half : half + low, :]], axis=0).T
+    out_o[:high, :] = buf[low:half, :]
+    out_o[high:, :] = buf[half + low :, :]
 
 
 def key_out_kernel(sizes, at, mine, other, out_k, out_v, *gains):
@@ -485,6 +501,7 @@
     heads = hq // hd
     scale = hd ** (-0.5)
     where = jnp.stack(S.sources() + [twin]).astype(jnp.int32)
+    members_from = jnp.stack(C.sources()).astype(jnp.int32)
     x = layer_input.reshape(rows, width)
     cot = out_cotangent.reshape(rows, width)
 
@@ -498,15 +515,12 @@
     gain_rows = jnp.concatenate([placed(small[:4]), placed(small[4:])], axis=0)
     gain_rows = jnp.pad(gain_rows, ((0, 8 - len(small)), (0, 0)))
 
-    whole = jnp.concatenate([w_query.T, w_key.T, w_value.T], axis=0)
+    whole = jnp.concatenate([w_query.T, w_key.T, w_value.T, w_output], axis=0)
     piece = whole.shape[0] // 2
     own = jnp.where(twin == 0, whole[:piece], whole[piece:])
     first = jnp.concatenate([own, gain_rows], axis=0)
     mine = S.gather(first)
     other = [C.send(m, 0, 1) for m in mine]
-    own = lax.dynamic_slice_in_dim(w_output, twin * (po // 2), po // 2, 0)
-    mine_o = S.gather(after(own, *mine[2::2]))
-    other_o = [C.send(m, 0, 1) for m in mine_o]
 
     pc = pf // members
 
@@ -514,7 +528,7 @@
         return lax.dynamic_slice_in_dim(w, C.rank * pc, pc, 0)
 
     ffn = jnp.concatenate([part_of(w_gate.T), part_of(w_up.T), part_of(w_down)], axis=0)
-    chunks = S.gather(after(ffn, *mine_o[2::2]))
+    chunks = S.gather(after(ffn, *mine[2::2]))
 
     places = seq_positions(block_pairs, span // 2)
     kpos = jnp.concatenate(
@@ -523,13 +537,18 @@
     own_pos = lax.dynamic_index_in_dim(places, C.rank, 1, keepdims=False).reshape(rows)
     cosine, sine = rope_tables(own_pos, hd)
     qpos = own_pos[:, None]
-
-    wq, wk, wv, gains, nin, qraw, kraw, qrot, kv = call(
+    key_at = jnp.stack([twin, S.rank]).astype(jnp.int32)
+    x, qpos, kpos, members_from, key_at = lax.optimization_barrier(
+        (x, qpos, kpos, members_from, key_at)
+    )
+
+    wq, wk, wv, wo, gains, nin, qraw, kraw, qrot, kv = call(
         functools.partial(qkv_kernel, count, heads),
         [
             ((hq, width), bf),
             ((hd, width), bf),
             ((hd, width), bf),
+            ((hq, width), bf),
             ((8, width), f32),
             ((rows, width), bf),
             ((rows, hq), f32),
@@ -542,8 +561,8 @@
     )
     kvs = C.gather(kv)
     length = members * span
-    att, probs, kall, proj, resid, nmid, wo = call(
-        functools.partial(attend_kernel, seqs, heads, scale, count),
+    att, probs, kall, proj, resid, nmid = call(
+        functools.partial(attend_kernel, seqs, heads, scale),
         [
             ((rows, hq), bf),
             ((seqs * heads * span, length), f32),
@@ -551,10 +570,8 @@
             ((rows, width), f32),
             ((rows, width), f32),
             ((rows, width), bf),
-            ((hq, width), bf),
         ],
-        (where, qpos, kpos, qrot, x, gains, *mine_o, *other_o, *kvs),
-        scalars=1,
+        (qpos, kpos, qrot, x, wo, gains, *kvs),
     )
     hid = count * pc
     wg, wu, wd, nm, gate, up, hidden, keep, give = call(
@@ -668,7 +685,18 @@
         scalars=1,
         scratch=[pltpu.VMEM((hq, width), f32), pltpu.VMEM((hq, width), f32)],
     )
-    q_terms = begin(keep, give, each_q)
+    q_got = C.send(give, 0, 1)
+    each_q //= C.outer
+    q_own, *q_gives = call(
+        functools.partial(part_kernel, C.outer, count),
+        [((count * each_q, width), f32)] + [((count * each_q, width), bf)] * (C.outer - 1),
+        ((C.rank // 2).astype(jnp.int32)[None], keep, q_got),
+        scalars=1,
+    )
+    for a, give in enumerate(q_gives):
+        q_own = q_own + C.send(give, a + 1, 0).astype(f32)
+    half = S.outer * each_q
+    q_terms = spread(q_own[:half], q_own[half:].astype(bf), each_q)
     input_grad, keep, give = call(
         functools.partial(key_back_kernel, count),
         [
@@ -701,27 +729,27 @@
         scratch=[pltpu.VMEM((hd, width), f32), pltpu.VMEM((hd, width), f32)],
     )
     k_terms = begin(keep, give, each_k)
-    total_q = finish(q_terms)
+    all_q = C.gather(summed(q_terms))
     total_k = finish(k_terms)
 
     out_gate, out_up, out_down = call(
         functools.partial(ffn_out_kernel, members),
         [((width, pf), f32), ((width, pf), f32), ((pf, width), f32)],
-        (jnp.stack(C.sources()).astype(jnp.int32), *C.gather(summed(f_terms))),
+        (members_from, *C.gather(summed(f_terms))),
         scalars=1,
         scratch=[pltpu.VMEM((pf, width), f32)],
     )
-    is_twin = twin.astype(jnp.int32)[None]
     out_query, out_output = call(
         functools.partial(query_out_kernel, (pq, po)),
         [((width, pq), f32), ((po, width), f32)],
-        (is_twin, *total_q),
+        (members_from, *all_q),
         scalars=1,
+        scratch=[pltpu.VMEM((pq + po, width), f32)],
     )
     out_key, out_value, *sums = call(
         functools.partial(key_out_kernel, (pk, pk)),
         [((pk, width), f32), ((pk, width), f32)] + [(g.shape, f32) for g in small],
-        (jnp.stack([twin, S.rank]).astype(jnp.int32), *total_k),
+        (key_at, *total_k),
         scalars=1,
     )
     out_key, out_value = out_key.T, out_value.T

time: 232 us -> 232 us (level)
  waiting for transfers between devices: 91.5 us -> 103 us
  starting transfers between devices: 52.6 us -> 41.7 us
    ppermute x73 -> x60, waiting for transfers between devices: 91.5 us -> 103 us  [send(): return lax.ppermute(x, self.name, pairs)]
    ppermute x73 -> x60, starting transfers between devices: 52.6 us -> 41.7 us  [send(): return lax.ppermute(x, self.name, pairs)]
    unnamed x142 -> x130, local copies, waits for them, and re-layouts: 14.4 us -> 14.6 us
  transfers between devices with their start and end apart: 73 -> 60, of which waited for: 26 -> 23; matrix products, arithmetic and copies ran while one was open for 5% -> 4% of each run, Pallas kernels for 14% -> 11%
where the time goes in v1:
time: 232 us; the launch traced here: 231 us
  waiting for transfers between devices  103 us (44%)
  Pallas kernels  56.7 us (24%)
  starting transfers between devices  41.7 us (18%)
  local copies, waits for them, and re-layouts  17.3 us (7%)
  other arithmetic  9.64 us (4%)
    ppermute x60, waiting for transfers between devices, send(): return lax.ppermute(x, self.name, pairs)  103 us
    pallas_call x17, Pallas kernels, call(): pl.pallas_call(body, out_shape=[jax.ShapeDtypeStruct(shape, kind) for sha...  56.7 us
    ppermute x60, starting transfers between devices, send(): return lax.ppermute(x, self.name, pairs)  41.7 us
    unnamed x130, local copies, waits for them, and re-layouts  14.6 us
  transfers between devices with their start and end apart: 60, of which 23 were waited for; matrix products, arithmetic and copies ran while one was open for 4% of the time, Pallas kernels for 11%

profile of v1, /device:TPU:0, one launch (start us, length us, event | category | flops | bytes accessed | tf_op | source)
XLA Modules:
  0.0 231.3 jit_solution(17984258280454028980)
XLA Ops:
  5.3 2.6 %collective-permute-start.10 = (bf16[168,640]{1,0:T(8,128)(2,1)S(1)}, bf16[168,640]{1,0:T(8,128)(2,1)S(1)}, u32[]{:S(2)}, u32[]{:S(2)}) collective-permute-start(bf16[168,640]{1,0:T(8,128)(2,1)S(1)} %pad_maximum_fusion.1.refs_0_), channel_id=1, source_target_pairs={{0,4},{4,0},{8,12},{12,8},{16,20},{20,16},{24,28},{28,24},{1,5},{5... | collective-permute-start | bytes 645128 | tf_op jit(solution)/shard_map/ppermute | solution.py:33
  7.8 3.6 %collective-permute-start.2 = (bf16[168,640]{1,0:T(8,128)(2,1)S(1)}, bf16[168,640]{1,0:T(8,128)(2,1)S(1)}, u32[]{:S(2)}, u32[]{:S(2)}) collective-permute-start(bf16[168,640]{1,0:T(8,128)(2,1)S(1)} %pad_maximum_fusion.1.refs_0_), channel_id=1, source_target_pairs={{0,24},{4,28},{8,0},{12,4},{16,8},{20,12},{24,16},{28,20},{1,25},{... | collective-permute-start | bytes 645128 | tf_op jit(solution)/shard_map/ppermute | solution.py:33
  18.0 12.0 %collective-permute-done.1.refs_4_ = bf16[168,640]{1,0:T(8,128)(2,1)S(1)} collective-permute-done((bf16[168,640]{1,0:T(8,128)(2,1)S(1)}, bf16[168,640]{1,0:T(8,128)(2,1)S(1)}, u32[]{:S(2)}, u32[]{:S(2)}) %collective-permute-start.1) | collective-permute-done | bytes 215072 | tf_op jit(solution)/shard_map/ppermute | solution.py:33
  32.8 5.4 %collective-permute-done.12.refs_5_ = bf16[168,640]{1,0:T(8,128)(2,1)S(1)} collective-permute-done((bf16[168,640]{1,0:T(8,128)(2,1)S(1)}, bf16[168,640]{1,0:T(8,128)(2,1)S(1)}, u32[]{:S(2)}, u32[]{:S(2)}) %collective-permute-start.12) | collective-permute-done | bytes 215072 | tf_op jit(solution)/shard_map/ppermute | solution.py:33
  38.2 2.9 %collective-permute-done.11.refs_3_ = bf16[168,640]{1,0:T(8,128)(2,1)S(1)} collective-permute-done((bf16[168,640]{1,0:T(8,128)(2,1)S(1)}, bf16[168,640]{1,0:T(8,128)(2,1)S(1)}, u32[]{:S(2)}, u32[]{:S(2)}) %collective-permute-start.11) | collective-permute-done | bytes 215072 | tf_op jit(solution)/shard_map/ppermute | solution.py:33
  43.6 4.5 %shard_map.271 = (bf16[1024,640]{1,0:T(8,128)(2,1)}, bf16[256,640]{1,0:T(8,128)(2,1)}, bf16[256,640]{1,0:T(8,128)(2,1)}, bf16[1024,640]{1,0:T(8,128)(2,1)}, f32[...) custom-call(s32[9]{0:T(128)} %stack.100.where, ...), custom_call_target="tpu_custom_call" | custom-call | tf_op jit(solution)/shard_map/pallas_call | solution.py:83
  52.1 2.3 collective-permute-done.23.refs_2_
  56.4 3.9 %shard_map.272 = (bf16[128,1024]{1,0:T(8,128)(2,1)}, f32[512,256]{1,0:T(8,128)}, bf16[512,512]{1,0:T(8,128)(2,1)}, f32[128,640]{1,0:T(8,128)}, f32[128,640]{1,0:T(8,128)}, /*index=5*/bf16[128,640]{1,0:T(8,128)(2,1)}) custom-call(s32[128,1]{1,0:T(8,128)} %copy.36.qpos, s32[2,256]{1,0:T(2,128)} %pad_add_fusion.kpos, ...), custom_call_target="tpu_custom_call" | custom-call | tf_op jit(solution)/shard_map/pallas_call | solution.py:83
  63.3 8.6 %collective-permute-done.6.refs_4_ = bf16[192,640]{1,0:T(8,128)(2,1)S(1)} collective-permute-done((bf16[192,640]{1,0:T(8,128)(2,1)S(1)}, bf16[192,640]{1,0:T(8,128)(2,1)S(1)}, u32[]{:S(2)}, u32[]{:S(2)}) %collective-permute-start.6) | collective-permute-done | bytes 245792 | tf_op jit(solution)/shard_map/ppermute | solution.py:33
  74.4 6.3 %collective-permute-done.7.refs_5_ = bf16[192,640]{1,0:T(8,128)(2,1)S(1)} collective-permute-done((bf16[192,640]{1,0:T(8,128)(2,1)S(1)}, bf16[192,640]{1,0:T(8,128)(2,1)S(1)}, u32[]{:S(2)}, u32[]{:S(2)}) %collective-permute-start.7) | collective-permute-done | bytes 245792 | tf_op jit(solution)/shard_map/ppermute | solution.py:33
  80.7 4.0 %collective-permute-done.5.refs_3_ = bf16[192,640]{1,0:T(8,128)(2,1)S(1)} collective-permute-done((bf16[192,640]{1,0:T(8,128)(2,1)S(1)}, bf16[192,640]{1,0:T(8,128)(2,1)S(1)}, u32[]{:S(2)}, u32[]{:S(2)}) %collective-permute-start.5) | collective-permute-done | bytes 245792 | tf_op jit(solution)/shard_map/ppermute | solution.py:33
  86.1 5.0 %shard_map.273 = (bf16[512,640]{1,0:T(8,128)(2,1)}, bf16[512,640]{1,0:T(8,128)(2,1)}, bf16[512,640]{1,0:T(8,128)(2,1)}, bf16[512,640]{1,0:T(8,128)(2,1)}, f32[51...) custom-call(bf16[192,640]{1,0:T(8,128)(2,1)} %copy-done.5, ...), custom_call_target="tpu_custom_call" | custom-call | tf_op jit(solution)/shard_map/pallas_call | solution.py:83
  94.7 5.7 %collective-permute-done.29.refs_0_ = bf16[128,640]{1,0:T(8,128)(2,1)S(1)} collective-permute-done((bf16[128,640]{1,0:T(8,128)(2,1)S(1)}, bf16[128,640]{1,0:T(8,128)(2,1)S(1)}, u32[]{:S(2)}, u32[]{:S(2)}) %collective-permute-start.29) | collective-permute-done | bytes 163872 | tf_op jit(solution)/shard_map/ppermute | solution.py:33
  101.1 2.4 %shard_map.274 = (bf16[128,640]{1,0:T(8,128)(2,1)}, bf16[128,640]{1,0:T(8,128)(2,1)}, f32[1,640]{1,0:T(1,128)}) custom-call(f32[256,640]{1,0:T(8,128)} %get-tuple-element.108.keep, bf16[256,640]{1,0:T(8,128)(2,1)} %copy-done.7, f32[128,640]{1,0:T(8,128)} %get-tuple-element.110.resid, bf16[128,640]{1,0:T(8,128)(2,1)} %bitcast.48, ...), custom_call_target="tpu_custom_call" | custom-call | tf_op jit(solution)/shard_map/pallas_call | solution.py:83
  104.0 5.1 %collective-permute-done.31.refs_2_ = bf16[128,640]{1,0:T(8,128)(2,1)S(1)} collective-permute-done((bf16[128,640]{1,0:T(8,128)(2,1)}, bf16[128,640]{1,0:T(8,128)(2,1)S(1)}, u32[]{:S(2)}, u32[]{:S(2)}) %collective-permute-start.31) | collective-permute-done | bytes 163872 | tf_op jit(solution)/shard_map/ppermute | solution.py:33
  111.1 5.3 %shard_map.275 = (bf16[512,640]{1,0:T(8,128)(2,1)}, bf16[512,512]{1,0:T(8,128)(2,1)}, bf16[512,512]{1,0:T(8,128)(2,1)}, f32[256,640]{1,0:T(8,128)}, bf16[256,640]{1,0:T(8,128)(2,1)}) custom-call(bf16[512,640]{1,0:T(8,128)(2,1)} %get-tuple-element.112.wg, bf16[512,640]{1,0:T(8,128)(2,1)} %get-tuple-element.113.wu, bf16[512,640]{1,0:T(8,128)(2,1)} %get-tuple-element.114.wd, ...), custom_call_target="tpu_custom_call" | custom-call | tf_op jit(solution)/shard_map/pallas_call | solution.py:83
  120.0 5.7 %collective-permute-done.34.refs_0_ = bf16[128,640]{1,0:T(8,128)(2,1)S(1)} collective-permute-done((bf16[128,640]{1,0:T(8,128)(2,1)S(1)}, bf16[128,640]{1,0:T(8,128)(2,1)S(1)}, u32[]{:S(2)}, u32[]{:S(2)}) %collective-permute-start.34) | collective-permute-done | bytes 163872 | tf_op jit(solution)/shard_map/ppermute | solution.py:33
  126.4 4.9 %shard_map.276 = (f32[128,640]{1,0:T(8,128)}, bf16[128,640]{1,0:T(8,128)(2,1)}, f32[128,1024]{1,0:T(8,128)}, f32[256,512]{1,0:T(8,128)}, bf16[256,512]{1,0:T(8,1...) custom-call(f32[256,640]{1,0:T(8,128)} %get-tuple-element.118.keep, bf16[256,640]{1,0:T(8,128)(2,1)} %copy-done.8, ...), custom_call_target="tpu_custom_call" | custom-call | tf_op jit(solution)/shard_map/pallas_call | solution.py:83
  131.2 4.3 %shard_map.277 = (bf16[128,1024]{1,0:T(8,128)(2,1)}, f32[1,256]{1,0:T(1,128)}, bf16[1024,640]{1,0:T(8,128)(2,1)}, bf16[1024,640]{1,0:T(8,128)(2,1)}) custom-call(s32[9]{0:T(128)} %stack.100.where, f32[128,1024]{1,0:T(8,128)} %get-tuple-element.127.dqrot, f32[128,1024]{1,0:T(8,128)} %get-tuple-element.128.qraw, f32[8,640]{1,0:T(8,128)} %get-tuple-element.105.gains, ...), custom_call_target="tpu_custom_call" | custom-call | tf_op jit(solution)/shard_map/pallas_call | solution.py:83
  135.5 3.2 %collective-permute-done.37.gave = bf16[1024,640]{1,0:T(8,128)(2,1)S(1)} collective-permute-done((bf16[1024,640]{1,0:T(8,128)(2,1)}, bf16[1024,640]{1,0:T(8,128)(2,1)S(1)}, u32[]{:S(2)}, u32[]{:S(2)}) %collective-permute-start.37) | collective-permute-done | bytes 1310752 | tf_op jit(solution)/shard_map/ppermute | solution.py:33
  139.9 3.2 %shard_map.279 = (f32[512,640]{1,0:T(8,128)}, bf16[512,640]{1,0:T(8,128)(2,1)}) custom-call(s32[1]{0:T(128)} %bitcast.33.outer, bf16[1024,640]{1,0:T(8,128)(2,1)} %get-tuple-element.142.keep, bf16[1024,640]{1,0:T(8,128)(2,1)} %copy-done.2), custom_call_target="tpu_custom_call" | custom-call | tf_op jit(solution)/shard_map/pallas_call | solution.py:83
  143.5 4.5 %shard_map.285 = (bf16[768,640]{1,0:T(8,128)(2,1)}, bf16[768,640]{1,0:T(8,128)(2,1)}) custom-call(bf16[512,640]{1,0:T(8,128)(2,1)} %get-tuple-element.163.nm, bf16[512,640]{1,0:T(8,128)(2,1)} %get-tuple-element.164.dall, bf16[512,512]{1,0:T(8,128)(2,1)} %get-tuple-element.165.dgate, bf16[512,512]{1,0:T(8,128)(2,1)} %get-tuple-element.166.dup, ...), custom_call_target="tpu_custom_call" | custom-call | tf_op jit(solution)/shard_map/pallas_call | solution.py:83
  150.2 12.6 %collective-permute-done.36.refs_0_ = bf16[128,512]{1,0:T(8,128)(2,1)S(1)} collective-permute-done((bf16[128,512]{1,0:T(8,128)(2,1)S(1)}, bf16[128,512]{1,0:T(8,128)(2,1)S(1)}, u32[]{:S(2)}, u32[]{:S(2)}) %collective-permute-start.36) | collective-permute-done | bytes 131104 | tf_op jit(solution)/shard_map/ppermute | solution.py:33
  163.5 4.0 %shard_map.278 = (f32[128,640]{1,0:T(8,128)}, f32[264,640]{1,0:T(8,128)}, bf16[264,640]{1,0:T(8,128)(2,1)}) custom-call(s32[9]{0:T(128)} %stack.100.where, f32[256,512]{1,0:T(8,128)} %get-tuple-element.123.kkeep, bf16[256,512]{1,0:T(8,128)(2,1)} %copy-done.10, f32[128,256]{1,0:T(8,128)} %get-tuple-element.125.kraw, f32[8,640]{1,0:T(8,128)} %get-tuple-element.105.gains, ...), custom_call_target="tpu_custom_call" | custom-call | tf_op jit(solution)/shard_map/pallas_call | solution.py:83
  170.2 2.3 collective-permute-done.53.gave
  172.5 2.7 %shard_map.286 = (f32[192,640]{1,0:T(8,128)}, bf16[192,640]{1,0:T(8,128)(2,1)}, bf16[192,640]{1,0:T(8,128)(2,1)}, bf16[192,640]{1,0:T(8,128)(2,1)}) custom-call(bf16[768,640]{1,0:T(8,128)(2,1)} %get-tuple-element.168.keep, bf16[768,640]{1,0:T(8,128)(2,1)} %collective-permute-done.53.gave), custom_call_target="tpu_custom_call" | custom-call | tf_op jit(solution)/shard_map/pallas_call | solution.py:83
  184.1 2.4 %collective-permute-start.40 = (bf16[64,640]{1,0:T(8,128)(2,1)}, bf16[64,640]{1,0:T(8,128)(2,1)S(1)}, u32[]{:S(2)}, u32[]{:S(2)}) collective-permute-start(bf16[64,640]{1,0:T(8,128)(2,1)} %get-tuple-element.147), channel_id=1, source_target_pairs={{0,24},{4,28},{8,0},{12,4},{16,8},{20,12},{24,16},{28,20},{1,25},{... | collective-permute-start | bytes 245768 | tf_op jit(solution)/shard_map/ppermute | solution.py:33
  187.1 12.4 %collective-permute-done.55 = bf16[192,640]{1,0:T(8,128)(2,1)} collective-permute-done((bf16[192,640]{1,0:T(8,128)(2,1)}, bf16[192,640]{1,0:T(8,128)(2,1)}, u32[]{:S(2)}, u32[]{:S(2)}) %collective-permute-start.55) | collective-permute-done | bytes 245792 | tf_op jit(solution)/shard_map/ppermute | solution.py:33
  205.1 3.8 %collective-permute-start.48 = (bf16[40,640]{1,0:T(8,128)(2,1)}, bf16[40,640]{1,0:T(8,128)(2,1)S(1)}, u32[]{:S(2)}, u32[]{:S(2)}) collective-permute-start(bf16[40,640]{1,0:T(8,128)(2,1)} %get-tuple-element.157), channel_id=1, source_target_pairs={{0,24},{4,28},{8,0},{12,4},{16,8},{20,12},{24,16},{28,20},{1,25},{... | collective-permute-start | bytes 153608 | tf_op jit(solution)/shard_map/ppermute | solution.py:33
  211.5 2.7 %collective-permute-done.49 = bf16[40,640]{1,0:T(8,128)(2,1)S(1)} collective-permute-done((bf16[40,640]{1,0:T(8,128)(2,1)}, bf16[40,640]{1,0:T(8,128)(2,1)S(1)}, u32[]{:S(2)}, u32[]{:S(2)}) %collective-permute-start.49) | collective-permute-done | bytes 51232 | tf_op jit(solution)/shard_map/ppermute | solution.py:33
  217.6 2.7 %collective-permute-done.51 = bf16[40,640]{1,0:T(8,128)(2,1)S(1)} collective-permute-done((bf16[40,640]{1,0:T(8,128)(2,1)S(1)}, bf16[40,640]{1,0:T(8,128)(2,1)S(1)}, u32[]{:S(2)}, u32[]{:S(2)}) %collective-permute-start.51) | collective-permute-done | bytes 51232 | tf_op jit(solution)/shard_map/ppermute | solution.py:33
  225.1 2.9 %shard_map.287 = (f32[640,256]{1,0:T(8,128)}, f32[640,256]{1,0:T(8,128)}, f32[256,640]{1,0:T(8,128)}) custom-call(s32[4]{0:T(128)} %pad_add_fusion.1.where, bf16[192,640]{1,0:T(8,128)(2,1)} %copy-done.4, bf16[192,640]{1,0:T(8,128)(2,1)} %copy-done.21, bf16[192,640]{1,0:T(8,128)(2,1)} %copy-done.15, bf16[192,640]{1,0:T(8,128)(2,1)} %copy-done.23), custom_call_target="tpu_custom_call" | custom-call | tf_op jit(solution)/shard_map/pallas_call | solution.py:83
  (270 shorter events, 76.2 us)
Async XLA Ops:
  4.7 12.5 %collective-permute-start.14 = (bf16[168,640]{1,0:T(8,128)(2,1)S(1)}, bf16[168,640]{1,0:T(8,128)(2,1)S(1)}, u32[]{:S(2)}, u32[]{:S(2)}) collective-permute-start(bf16[168,640]{1,0:T(8,128)(2,1)S(1)} %pad_maximum_fusion.1.refs_0_), channel_id=1, source_target_pairs={{0,1},{1,0},{2,3},{3,2},{4,5},{5,4},{6,7},{7,6},{8,9},{9,8},{10,11... | collective-permute-start | bytes 645128 | tf_op jit(solution)/shard_map/ppermute | solution.py:33
  5.3 12.5 %collective-permute-start.10 = (bf16[168,640]{1,0:T(8,128)(2,1)S(1)}, bf16[168,640]{1,0:T(8,128)(2,1)S(1)}, u32[]{:S(2)}, u32[]{:S(2)}) collective-permute-start(bf16[168,640]{1,0:T(8,128)(2,1)S(1)} %pad_maximum_fusion.1.refs_0_), channel_id=1, source_target_pairs={{0,4},{4,0},{8,12},{12,8},{16,20},{20,16},{24,28},{28,24},{1,5},{5... | collective-permute-start | bytes 645128 | tf_op jit(solution)/shard_map/ppermute | solution.py:33
  11.4 18.6 %collective-permute-start.1 = (bf16[168,640]{1,0:T(8,128)(2,1)S(1)}, bf16[168,640]{1,0:T(8,128)(2,1)S(1)}, u32[]{:S(2)}, u32[]{:S(2)}) collective-permute-start(bf16[168,640]{1,0:T(8,128)(2,1)S(1)} %pad_maximum_fusion.1.refs_0_), channel_id=1, source_target_pairs={{0,16},{4,20},{8,24},{12,28},{16,0},{20,4},{24,8},{28,12},{1,17},{... | collective-permute-start | bytes 645128 | tf_op jit(solution)/shard_map/ppermute | solution.py:33
  11.4 19.1 %collective-permute-start = (bf16[168,640]{1,0:T(8,128)(2,1)S(1)}, bf16[168,640]{1,0:T(8,128)(2,1)S(1)}, u32[]{:S(2)}, u32[]{:S(2)}) collective-permute-start(bf16[168,640]{1,0:T(8,128)(2,1)S(1)} %pad_maximum_fusion.1.refs_0_), channel_id=1, source_target_pairs={{0,8},{4,12},{8,16},{12,20},{16,24},{20,28},{24,0},{28,4},{1,9},{5... | collective-permute-start | bytes 645128 | tf_op jit(solution)/shard_map/ppermute | solution.py:33
  17.2 15.0 %collective-permute-start.20 = (bf16[168,640]{1,0:T(8,128)(2,1)S(1)}, bf16[168,640]{1,0:T(8,128)(2,1)S(1)}, u32[]{:S(2)}, u32[]{:S(2)}) collective-permute-start(bf16[168,640]{1,0:T(8,128)(2,1)S(1)} %collective-permute-done.2.refs_6_), channel_id=1, source_target_pairs={{0,1},{1,0},{2,3},{3,2},{4,5},{5,4},{6,7},{7,6},{8,9},{9,8},{10,11... | collective-permute-start | bytes 645128 | tf_op jit(solution)/shard_map/ppermute | solution.py:33
  17.2 15.5 %collective-permute-start.13 = (bf16[168,640]{1,0:T(8,128)(2,1)S(1)}, bf16[168,640]{1,0:T(8,128)(2,1)S(1)}, u32[]{:S(2)}, u32[]{:S(2)}) collective-permute-start(bf16[168,640]{1,0:T(8,128)(2,1)S(1)} %collective-permute-done.2.refs_6_), channel_id=1, source_target_pairs={{0,4},{4,0},{8,12},{12,8},{16,20},{20,16},{24,28},{28,24},{1,5},{5... | collective-permute-start | bytes 645128 | tf_op jit(solution)/shard_map/ppermute | solution.py:33
  17.8 14.3 %collective-permute-start.15 = (bf16[168,640]{1,0:T(8,128)(2,1)S(1)}, bf16[168,640]{1,0:T(8,128)(2,1)S(1)}, u32[]{:S(2)}, u32[]{:S(2)}) collective-permute-start(bf16[168,640]{1,0:T(8,128)(2,1)S(1)} %collective-permute-done.10.refs_1_), channel_id=1, source_target_pairs={{0,1},{1,0},{2,3},{3,2},{4,5},{5,4},{6,7},{7,6},{8,9},{9,8},{10,11... | collective-permute-start | bytes 645128 | tf_op jit(solution)/shard_map/ppermute | solution.py:33
  30.6 10.6 %collective-permute-start.11 = (bf16[168,640]{1,0:T(8,128)(2,1)S(1)}, bf16[168,640]{1,0:T(8,128)(2,1)S(1)}, u32[]{:S(2)}, u32[]{:S(2)}) collective-permute-start(bf16[168,640]{1,0:T(8,128)(2,1)S(1)} %collective-permute-done.refs_2_), channel_id=1, source_target_pairs={{0,4},{4,0},{8,12},{12,8},{16,20},{20,16},{24,28},{28,24},{1,5},{5... | collective-permute-start | bytes 645128 | tf_op jit(solution)/shard_map/ppermute | solution.py:33
  32.1 10.0 %collective-permute-start.18 = (bf16[168,640]{1,0:T(8,128)(2,1)S(1)}, bf16[168,640]{1,0:T(8,128)(2,1)S(1)}, u32[]{:S(2)}, u32[]{:S(2)}) collective-permute-start(bf16[168,640]{1,0:T(8,128)(2,1)S(1)} %collective-permute-done.1.refs_4_), channel_id=1, source_target_pairs={{0,1},{1,0},{2,3},{3,2},{4,5},{5,4},{6,7},{7,6},{8,9},{9,8},{10,11... | collective-permute-start | bytes 645128 | tf_op jit(solution)/shard_map/ppermute | solution.py:33
  50.0 11.7 %collective-permute-start.8 = (bf16[192,640]{1,0:T(8,128)(2,1)S(1)}, bf16[192,640]{1,0:T(8,128)(2,1)S(1)}, u32[]{:S(2)}, u32[]{:S(2)}) collective-permute-start(bf16[192,640]{1,0:T(8,128)(2,1)S(1)} %pad_maximum_fusion.refs_0_), channel_id=1, source_target_pairs={{0,24},{4,28},{8,0},{12,4},{16,8},{20,12},{24,16},{28,20},{1,25},{... | collective-permute-start | bytes 737288 | tf_op jit(solution)/shard_map/ppermute | solution.py:33
  50.1 21.7 %collective-permute-start.6 = (bf16[192,640]{1,0:T(8,128)(2,1)S(1)}, bf16[192,640]{1,0:T(8,128)(2,1)S(1)}, u32[]{:S(2)}, u32[]{:S(2)}) collective-permute-start(bf16[192,640]{1,0:T(8,128)(2,1)S(1)} %pad_maximum_fusion.refs_0_), channel_id=1, source_target_pairs={{0,16},{4,20},{8,24},{12,28},{16,0},{20,4},{24,8},{28,12},{1,17},{... | collective-permute-start | bytes 737288 | tf_op jit(solution)/shard_map/ppermute | solution.py:33
  50.2 22.2 %collective-permute-start.4 = (bf16[192,640]{1,0:T(8,128)(2,1)S(1)}, bf16[192,640]{1,0:T(8,128)(2,1)S(1)}, u32[]{:S(2)}, u32[]{:S(2)}) collective-permute-start(bf16[192,640]{1,0:T(8,128)(2,1)S(1)} %pad_maximum_fusion.refs_0_), channel_id=1, source_target_pairs={{0,8},{4,12},{8,16},{12,20},{16,24},{20,28},{24,0},{28,4},{1,9},{5... | collective-permute-start | bytes 737288 | tf_op jit(solution)/shard_map/ppermute | solution.py:33
  54.4 19.5 %collective-permute-start.3 = (bf16[192,640]{1,0:T(8,128)(2,1)S(1)}, bf16[192,640]{1,0:T(8,128)(2,1)S(1)}, u32[]{:S(2)}, u32[]{:S(2)}) collective-permute-start(bf16[192,640]{1,0:T(8,128)(2,1)S(1)} %pad_maximum_fusion.refs_0_), channel_id=1, source_target_pairs={{0,4},{4,0},{8,12},{12,8},{16,20},{20,16},{24,28},{28,24},{1,5},{5... | collective-permute-start | bytes 737288 | tf_op jit(solution)/shard_map/ppermute | solution.py:33
  60.2 13.6 %collective-permute-start.26 = (bf16[128,640]{1,0:T(8,128)(2,1)}, bf16[128,640]{1,0:T(8,128)(2,1)S(1)}, u32[]{:S(2)}, u32[]{:S(2)}) collective-permute-start(bf16[128,640]{1,0:T(8,128)(2,1)} %get-tuple-element.107.refs_8_), channel_id=1, source_target_pairs={{0,2},{1,3},{2,0},{3,1},{4,6},{5,7},{6,4},{7,5},{8,10},{9,11},{10,... | collective-permute-start | bytes 491528 | tf_op jit(solution)/shard_map/ppermute | solution.py:33
  61.8 12.6 %collective-permute-start.9 = (bf16[192,640]{1,0:T(8,128)(2,1)S(1)}, bf16[192,640]{1,0:T(8,128)(2,1)S(1)}, u32[]{:S(2)}, u32[]{:S(2)}) collective-permute-start(bf16[192,640]{1,0:T(8,128)(2,1)S(1)} %collective-permute-done.8.refs_6_), channel_id=1, source_target_pairs={{0,4},{4,0},{8,12},{12,8},{16,20},{20,16},{24,28},{28,24},{1,5},{5... | collective-permute-start | bytes 737288 | tf_op jit(solution)/shard_map/ppermute | solution.py:33
  72.4 12.3 %collective-permute-start.5 = (bf16[192,640]{1,0:T(8,128)(2,1)S(1)}, bf16[192,640]{1,0:T(8,128)(2,1)S(1)}, u32[]{:S(2)}, u32[]{:S(2)}) collective-permute-start(bf16[192,640]{1,0:T(8,128)(2,1)S(1)} %collective-permute-done.4.refs_2_), channel_id=1, source_target_pairs={{0,4},{4,0},{8,12},{12,8},{16,20},{20,16},{24,28},{28,24},{1,5},{5... | collective-permute-start | bytes 737288 | tf_op jit(solution)/shard_map/ppermute | solution.py:33
  73.9 10.8 %collective-permute-start.25 = (bf16[128,640]{1,0:T(8,128)(2,1)}, bf16[128,640]{1,0:T(8,128)(2,1)S(1)}, u32[]{:S(2)}, u32[]{:S(2)}) collective-permute-start(bf16[128,640]{1,0:T(8,128)(2,1)} %get-tuple-element.107.refs_8_), channel_id=1, source_target_pairs={{0,1},{1,0},{2,3},{3,2},{4,5},{5,4},{6,7},{7,6},{8,9},{9,8},{10,11... | collective-permute-start | bytes 491528 | tf_op jit(solution)/shard_map/ppermute | solution.py:33
  73.9 10.8 %collective-permute-start.27 = (bf16[128,640]{1,0:T(8,128)(2,1)S(1)}, bf16[128,640]{1,0:T(8,128)(2,1)S(1)}, u32[]{:S(2)}, u32[]{:S(2)}) collective-permute-start(bf16[128,640]{1,0:T(8,128)(2,1)S(1)} %collective-permute-done.26.refs_10_), channel_id=1, source_target_pairs={{0,1},{1,0},{2,3},{3,2},{4,5},{5,4},{6,7},{7,6},{8,9},{9,8},{10,11... | collective-permute-start | bytes 491528 | tf_op jit(solution)/shard_map/ppermute | solution.py:33
  143.0 24.5 %collective-permute-start.38 = (bf16[512,640]{1,0:T(8,128)(2,1)}, bf16[512,640]{1,0:T(8,128)(2,1)S(1)}, u32[]{:S(2)}, u32[]{:S(2)}) collective-permute-start(bf16[512,640]{1,0:T(8,128)(2,1)} %get-tuple-element.145), channel_id=1, source_target_pairs={{0,2},{1,3},{2,0},{3,1},{4,6},{5,7},{6,4},{7,5},{8,10},{9,11},{10,... | collective-permute-start | bytes 1966088 | tf_op jit(solution)/shard_map/ppermute | solution.py:33
  148.0 24.5 %collective-permute-start.53 = (bf16[768,640]{1,0:T(8,128)(2,1)}, bf16[768,640]{1,0:T(8,128)(2,1)}, u32[]{:S(2)}, u32[]{:S(2)}) collective-permute-start(bf16[768,640]{1,0:T(8,128)(2,1)} %get-tuple-element.169), channel_id=1, source_target_pairs={{0,4},{4,0},{8,12},{12,8},{16,20},{20,16},{24,28},{28,24},{1,5},{5... | collective-permute-start | bytes 2949128 | tf_op jit(solution)/shard_map/ppermute | solution.py:33
  148.6 14.2 %collective-permute-start.36 = (bf16[128,512]{1,0:T(8,128)(2,1)S(1)}, bf16[128,512]{1,0:T(8,128)(2,1)S(1)}, u32[]{:S(2)}, u32[]{:S(2)}) collective-permute-start(bf16[128,512]{1,0:T(8,128)(2,1)S(1)} %add_convert_fusion.3), channel_id=1, source_target_pairs={{0,2},{1,3},{2,0},{3,1},{4,6},{5,7},{6,4},{7,5},{8,10},{9,11},{10,... | collective-permute-start | bytes 393224 | tf_op jit(solution)/shard_map/ppermute | solution.py:33
  169.6 11.8 %collective-permute-start.39 = (bf16[256,640]{1,0:T(8,128)(2,1)S(1)}, bf16[256,640]{1,0:T(8,128)(2,1)S(1)}, u32[]{:S(2)}, u32[]{:S(2)}) collective-permute-start(bf16[256,640]{1,0:T(8,128)(2,1)S(1)} %slice.49), channel_id=1, source_target_pairs={{0,4},{4,0},{8,12},{12,8},{16,20},{20,16},{24,28},{28,24},{1,5},{5... | collective-permute-start | bytes 983048 | tf_op jit(solution)/shard_map/ppermute | solution.py:33
  175.2 11.2 %collective-permute-start.54 = (bf16[192,640]{1,0:T(8,128)(2,1)}, bf16[192,640]{1,0:T(8,128)(2,1)S(1)}, u32[]{:S(2)}, u32[]{:S(2)}) collective-permute-start(bf16[192,640]{1,0:T(8,128)(2,1)} %get-tuple-element.171), channel_id=1, source_target_pairs={{0,24},{4,28},{8,0},{12,4},{16,8},{20,12},{24,16},{28,20},{1,25},{... | collective-permute-start | bytes 737288 | tf_op jit(solution)/shard_map/ppermute | solution.py:33
  175.2 24.3 %collective-permute-start.55 = (bf16[192,640]{1,0:T(8,128)(2,1)}, bf16[192,640]{1,0:T(8,128)(2,1)}, u32[]{:S(2)}, u32[]{:S(2)}) collective-permute-start(bf16[192,640]{1,0:T(8,128)(2,1)} %get-tuple-element.172), channel_id=1, source_target_pairs={{0,16},{4,20},{8,24},{12,28},{16,0},{20,4},{24,8},{28,12},{1,17},{... | collective-permute-start | bytes 737288 | tf_op jit(solution)/shard_map/ppermute | solution.py:33
  175.2 24.3 %collective-permute-start.56 = (bf16[192,640]{1,0:T(8,128)(2,1)}, bf16[192,640]{1,0:T(8,128)(2,1)}, u32[]{:S(2)}, u32[]{:S(2)}) collective-permute-start(bf16[192,640]{1,0:T(8,128)(2,1)} %get-tuple-element.173), channel_id=1, source_target_pairs={{0,8},{4,12},{8,16},{12,20},{16,24},{20,28},{24,0},{28,4},{1,9},{5... | collective-permute-start | bytes 737288 | tf_op jit(solution)/shard_map/ppermute | solution.py:33
  180.0 22.8 %collective-permute-start.47 = (bf16[136,640]{1,0:T(8,128)(2,1)}, bf16[136,640]{1,0:T(8,128)(2,1)S(1)}, u32[]{:S(2)}, u32[]{:S(2)}) collective-permute-start(bf16[136,640]{1,0:T(8,128)(2,1)} %get-tuple-element.155), channel_id=1, source_target_pairs={{0,4},{4,0},{8,12},{12,8},{16,20},{20,16},{24,28},{28,24},{1,5},{5... | collective-permute-start | bytes 522248 | tf_op jit(solution)/shard_map/ppermute | solution.py:33
  184.1 24.9 %collective-permute-start.40 = (bf16[64,640]{1,0:T(8,128)(2,1)}, bf16[64,640]{1,0:T(8,128)(2,1)S(1)}, u32[]{:S(2)}, u32[]{:S(2)}) collective-permute-start(bf16[64,640]{1,0:T(8,128)(2,1)} %get-tuple-element.147), channel_id=1, source_target_pairs={{0,24},{4,28},{8,0},{12,4},{16,8},{20,12},{24,16},{28,20},{1,25},{... | collective-permute-start | bytes 245768 | tf_op jit(solution)/shard_map/ppermute | solution.py:33
  186.4 22.5 %collective-permute-start.41 = (bf16[64,640]{1,0:T(8,128)(2,1)}, bf16[64,640]{1,0:T(8,128)(2,1)S(1)}, u32[]{:S(2)}, u32[]{:S(2)}) collective-permute-start(bf16[64,640]{1,0:T(8,128)(2,1)} %get-tuple-element.148), channel_id=1, source_target_pairs={{0,16},{4,20},{8,24},{12,28},{16,0},{20,4},{24,8},{28,12},{1,17},{... | collective-permute-start | bytes 245768 | tf_op jit(solution)/shard_map/ppermute | solution.py:33
  199.5 11.4 %collective-permute-start.42 = (bf16[64,640]{1,0:T(8,128)(2,1)}, bf16[64,640]{1,0:T(8,128)(2,1)S(1)}, u32[]{:S(2)}, u32[]{:S(2)}) collective-permute-start(bf16[64,640]{1,0:T(8,128)(2,1)} %get-tuple-element.149), channel_id=1, source_target_pairs={{0,8},{4,12},{8,16},{12,20},{16,24},{20,28},{24,0},{28,4},{1,9},{5... | collective-permute-start | bytes 245768 | tf_op jit(solution)/shard_map/ppermute | solution.py:33
  200.7 15.9 %collective-permute-start.58 = (bf16[192,640]{1,0:T(8,128)(2,1)S(1)}, bf16[192,640]{1,0:T(8,128)(2,1)S(1)}, u32[]{:S(2)}, u32[]{:S(2)}) collective-permute-start(bf16[192,640]{1,0:T(8,128)(2,1)S(1)} %add_convert_fusion.refs_0_), channel_id=1, source_target_pairs={{0,2},{1,3},{2,0},{3,1},{4,6},{5,7},{6,4},{7,5},{8,10},{9,11},{10,... | collective-permute-start | bytes 737288 | tf_op jit(solution)/shard_map/ppermute | solution.py:33
  217.1 11.0 %collective-permute-start.43 = (bf16[64,640]{1,0:T(8,128)(2,1)S(1)}, bf16[64,640]{1,0:T(8,128)(2,1)S(1)}, u32[]{:S(2)}, u32[]{:S(2)}) collective-permute-start(bf16[64,640]{1,0:T(8,128)(2,1)S(1)} %add_convert_fusion.4.refs_0_), channel_id=1, source_target_pairs={{0,1},{1,0},{2,3},{3,2},{4,5},{5,4},{6,7},{7,6},{8,9},{9,8},{10,11... | collective-permute-start | bytes 245768 | tf_op jit(solution)/shard_map/ppermute | solution.py:33
  217.1 10.9 %collective-permute-start.45 = (bf16[64,640]{1,0:T(8,128)(2,1)S(1)}, bf16[64,640]{1,0:T(8,128)(2,1)S(1)}, u32[]{:S(2)}, u32[]{:S(2)}) collective-permute-start(bf16[64,640]{1,0:T(8,128)(2,1)S(1)} %collective-permute-done.44.refs_2_), channel_id=1, source_target_pairs={{0,1},{1,0},{2,3},{3,2},{4,5},{5,4},{6,7},{7,6},{8,9},{9,8},{10,11... | collective-permute-start | bytes 245768 | tf_op jit(solution)/shard_map/ppermute | solution.py:33
  (91 other events, 701.0 us)

commit v2 on v1

--- a/solution.py
+++ b/solution.py
@@ -109,13 +109,14 @@
     return lax.optimization_barrier((x,) + deps)[0]
 
 
-def unpack(where, mine, other, piece, outs):
+def unpack(where, mine, other, piece, outs, start=0):
     count = len(mine)
+    first = start
 
     def put(low, high):
         for i in range(count):
             block = where[i]
-            start = 0
+            start = first
             for out in outs:
                 size = out.shape[0] // count
                 for at, ref in ((0, low[i]), (piece, high[i])):
@@ -136,10 +137,10 @@
 
 def qkv_kernel(count, heads, where, x, cosine, sine, *refs):
     mine, other = refs[:count], refs[count : 2 * count]
-    wq, wk, wv, wo, gains, nin, qraw, kraw, qrot, kv = refs[2 * count :]
-    piece = sum(w.shape[0] for w in (wq, wk, wv, wo)) // count // 2
+    wq, wk, wv, gains, nin, qraw, kraw, qrot, kv = refs[2 * count :]
+    piece = mine[0].shape[0] - 8
     hd = wk.shape[0]
-    unpack(where, mine, other, piece, (wq, wk, wv, wo))
+    unpack(where, mine, other, piece, (wq, wk, wv))
     total = mine[0][piece:, :].astype(f32)
     for i in range(1, count):
         total = total + mine[i][piece:, :].astype(f32)
@@ -165,6 +166,11 @@
     kv[:, :half] = a.astype(bf)
     kv[:, half:hd] = b.astype(bf)
     kv[:, hd:] = times_t(normed, wv[...]).astype(bf)
+
+
+def output_weight_kernel(count, start, where, *refs):
+    mine, other = refs[:count], refs[count : 2 * count]
+    unpack(where, mine, other, mine[0].shape[0] - 8, refs[2 * count :], start)
 
 
 def stacked(ref, rows, heads, hd):
@@ -221,8 +227,8 @@
         nm[i * rows : (i + 1) * rows, :] = blocks[i][...]
     g = times_t(nm[...], wg[...])
     u = times_t(nm[...], wu[...])
-    gate[...] = g
-    up[...] = u
+    gate[...] = g.astype(bf)
+    up[...] = u.astype(bf)
     t = jnp.tanh(root * (g + cubic * (g * g * g)))
     hid = (0.5 * g * (1.0 + t) * u).astype(bf)
     hidden[...] = hid
@@ -248,7 +254,7 @@
     for i in range(members):
         dall[i * rows : (i + 1) * rows, :] = blocks[i][...]
     d_hidden = times_t(dall[...], wd[...])
-    g, u = gate[...], up[...]
+    g, u = gate[...].astype(f32), up[...].astype(f32)
     t = jnp.tanh(root * (g + cubic * (g * g * g)))
     slope = 0.5 * (1.0 + t) + 0.5 * g * (1.0 - t * t) * (root * (1.0 + 3.0 * cubic * (g * g)))
     dg = (d_hidden * u * slope).astype(bf)
@@ -542,13 +548,12 @@
         (x, qpos, kpos, members_from, key_at)
     )
 
-    wq, wk, wv, wo, gains, nin, qraw, kraw, qrot, kv = call(
+    wq, wk, wv, gains, nin, qraw, kraw, qrot, kv = call(
         functools.partial(qkv_kernel, count, heads),
         [
             ((hq, width), bf),
             ((hd, width), bf),
             ((hd, width), bf),
-            ((hq, width), bf),
             ((8, width), f32),
             ((rows, width), bf),
             ((rows, hq), f32),
@@ -560,6 +565,12 @@
         scalars=1,
     )
     kvs = C.gather(kv)
+    (wo,) = call(
+        functools.partial(output_weight_kernel, count, pq + 2 * pk),
+        [((hq, width), bf)],
+        (where, *mine, *other),
+        scalars=1,
+    )
     length = members * span
     att, probs, kall, proj, resid, nmid = call(
         functools.partial(attend_kernel, seqs, heads, scale),
@@ -581,8 +592,8 @@
             ((hid, width), bf),
             ((hid, width), bf),
             ((members * rows, width), bf),
-            ((members * rows, hid), f32),
-            ((members * rows, hid), f32),
+            ((members * rows, hid), bf),
+            ((members * rows, hid), bf),
             ((members * rows, hid), bf),
             ((C.outer * rows, width), f32),
             ((C.outer * rows, width), bf),

time: 232 us -> 232 us (level)
  waiting for transfers between devices: 103 us -> 99.1 us
    ppermute x60, waiting for transfers between devices: 103 us -> 99.1 us  [send(): return lax.ppermute(x, self.name, pairs)]
    pallas_call x17 -> x18, Pallas kernels: 56.7 us -> 58.7 us  [call(): pl.pallas_call(body, out_shape=[jax.ShapeDtypeStruct(shape, kind) for sha...]
  transfers between devices with their start and end apart: 60 -> 60, of which waited for: 23 -> 23; matrix products, arithmetic and copies ran while one was open for 4% -> 5% of each run, Pallas kernels for 11% -> 12%
where the time goes in v2:
time: 232 us; the launch traced here: 231 us
  waiting for transfers between devices  99.1 us (43%)
  Pallas kernels  58.7 us (25%)
  starting transfers between devices  41.4 us (18%)
  local copies, waits for them, and re-layouts  18 us (8%)
  other arithmetic  10.6 us (5%)
    ppermute x60, waiting for transfers between devices, send(): return lax.ppermute(x, self.name, pairs)  99.1 us
    pallas_call x18, Pallas kernels, call(): pl.pallas_call(body, out_shape=[jax.ShapeDtypeStruct(shape, kind) for sha...  58.7 us
    ppermute x60, starting transfers between devices, send(): return lax.ppermute(x, self.name, pairs)  41.4 us
    unnamed x130, local copies, waits for them, and re-layouts  15.3 us
  transfers between devices with their start and end apart: 60, of which 23 were waited for; matrix products, arithmetic and copies ran while one was open for 5% of the time, Pallas kernels for 12%

profile of v2, /device:TPU:0, one launch (start us, length us, event | category | flops | bytes accessed | tf_op | source)
XLA Modules:
  0.0 230.9 jit_solution(5164907352897510266)
XLA Ops:
  5.3 2.6 %collective-permute-start.10 = (bf16[168,640]{1,0:T(8,128)(2,1)S(1)}, bf16[168,640]{1,0:T(8,128)(2,1)S(1)}, u32[]{:S(2)}, u32[]{:S(2)}) collective-permute-start(bf16[168,640]{1,0:T(8,128)(2,1)S(1)} %pad_maximum_fusion.1.refs_0_), channel_id=1, source_target_pairs={{0,4},{4,0},{8,12},{12,8},{16,20},{20,16},{24,28},{28,24},{1,5},{5... | collective-permute-start | bytes 645128 | tf_op jit(solution)/shard_map/ppermute | solution.py:33
  7.8 3.6 %collective-permute-start.2 = (bf16[168,640]{1,0:T(8,128)(2,1)S(1)}, bf16[168,640]{1,0:T(8,128)(2,1)S(1)}, u32[]{:S(2)}, u32[]{:S(2)}) collective-permute-start(bf16[168,640]{1,0:T(8,128)(2,1)S(1)} %pad_maximum_fusion.1.refs_0_), channel_id=1, source_target_pairs={{0,24},{4,28},{8,0},{12,4},{16,8},{20,12},{24,16},{28,20},{1,25},{... | collective-permute-start | bytes 645128 | tf_op jit(solution)/shard_map/ppermute | solution.py:33
  18.0 12.0 %collective-permute-done.1.refs_4_ = bf16[168,640]{1,0:T(8,128)(2,1)S(1)} collective-permute-done((bf16[168,640]{1,0:T(8,128)(2,1)S(1)}, bf16[168,640]{1,0:T(8,128)(2,1)S(1)}, u32[]{:S(2)}, u32[]{:S(2)}) %collective-permute-start.1) | collective-permute-done | bytes 215072 | tf_op jit(solution)/shard_map/ppermute | solution.py:33
  32.8 5.4 %collective-permute-done.12.refs_5_ = bf16[168,640]{1,0:T(8,128)(2,1)S(1)} collective-permute-done((bf16[168,640]{1,0:T(8,128)(2,1)S(1)}, bf16[168,640]{1,0:T(8,128)(2,1)S(1)}, u32[]{:S(2)}, u32[]{:S(2)}) %collective-permute-start.12) | collective-permute-done | bytes 215072 | tf_op jit(solution)/shard_map/ppermute | solution.py:33
  38.2 2.9 %collective-permute-done.11.refs_3_ = bf16[168,640]{1,0:T(8,128)(2,1)S(1)} collective-permute-done((bf16[168,640]{1,0:T(8,128)(2,1)S(1)}, bf16[168,640]{1,0:T(8,128)(2,1)S(1)}, u32[]{:S(2)}, u32[]{:S(2)}) %collective-permute-start.11) | collective-permute-done | bytes 215072 | tf_op jit(solution)/shard_map/ppermute | solution.py:33
  43.7 4.0 %shard_map.271 = (bf16[1024,640]{1,0:T(8,128)(2,1)}, bf16[256,640]{1,0:T(8,128)(2,1)}, bf16[256,640]{1,0:T(8,128)(2,1)}, f32[8,640]{1,0:T(8,128)}, bf16[128,640]...) custom-call(s32[9]{0:T(128)} %stack.100.where, ...), custom_call_target="tpu_custom_call" | custom-call | tf_op jit(solution)/shard_map/pallas_call | solution.py:83
  55.3 3.4 %shard_map.272.wo = bf16[1024,640]{1,0:T(8,128)(2,1)} custom-call(s32[9]{0:T(128)} %stack.100.where, bf16[168,640]{1,0:T(8,128)(2,1)} %copy-done.1, bf16[168,640]{1,0:T(8,128)(2,1)} %copy-done.8, bf16[168,640]{1,0:T(8,128)(2,1)} %copy-done.11, bf16[168,640]{1,0:T(8,128)(2,1)} %copy-done.16, bf16[168,640]{1,0:T(8,128)(2,1)} %copy-done.10, ...), custom_call_target="tpu_custom_call" | custom-call | tf_op jit(solution)/shard_map/pallas_call | solution.py:83
  59.4 3.9 %shard_map.273 = (bf16[128,1024]{1,0:T(8,128)(2,1)}, f32[512,256]{1,0:T(8,128)}, bf16[512,512]{1,0:T(8,128)(2,1)}, f32[128,640]{1,0:T(8,128)}, f32[128,640]{1,0:T(8,128)}, /*index=5*/bf16[128,640]{1,0:T(8,128)(2,1)}) custom-call(s32[128,1]{1,0:T(8,128)} %copy.36.qpos, s32[2,256]{1,0:T(2,128)} %pad_add_fusion.kpos, ...), custom_call_target="tpu_custom_call" | custom-call | tf_op jit(solution)/shard_map/pallas_call | solution.py:83
  66.3 6.0 %collective-permute-done.6.refs_4_ = bf16[192,640]{1,0:T(8,128)(2,1)S(1)} collective-permute-done((bf16[192,640]{1,0:T(8,128)(2,1)S(1)}, bf16[192,640]{1,0:T(8,128)(2,1)S(1)}, u32[]{:S(2)}, u32[]{:S(2)}) %collective-permute-start.6) | collective-permute-done | bytes 245792 | tf_op jit(solution)/shard_map/ppermute | solution.py:33
  74.8 6.3 %collective-permute-done.7.refs_5_ = bf16[192,640]{1,0:T(8,128)(2,1)S(1)} collective-permute-done((bf16[192,640]{1,0:T(8,128)(2,1)S(1)}, bf16[192,640]{1,0:T(8,128)(2,1)S(1)}, u32[]{:S(2)}, u32[]{:S(2)}) %collective-permute-start.7) | collective-permute-done | bytes 245792 | tf_op jit(solution)/shard_map/ppermute | solution.py:33
  81.1 4.0 %collective-permute-done.5.refs_3_ = bf16[192,640]{1,0:T(8,128)(2,1)S(1)} collective-permute-done((bf16[192,640]{1,0:T(8,128)(2,1)S(1)}, bf16[192,640]{1,0:T(8,128)(2,1)S(1)}, u32[]{:S(2)}, u32[]{:S(2)}) %collective-permute-start.5) | collective-permute-done | bytes 245792 | tf_op jit(solution)/shard_map/ppermute | solution.py:33
  86.6 4.6 %shard_map.274 = (bf16[512,640]{1,0:T(8,128)(2,1)}, bf16[512,640]{1,0:T(8,128)(2,1)}, bf16[512,640]{1,0:T(8,128)(2,1)}, bf16[512,640]{1,0:T(8,128)(2,1)}, bf16[5...) custom-call(bf16[192,640]{1,0:T(8,128)(2,1)} %copy-done.6, ...), custom_call_target="tpu_custom_call" | custom-call | tf_op jit(solution)/shard_map/pallas_call | solution.py:83
  94.7 5.7 %collective-permute-done.29.refs_0_ = bf16[128,640]{1,0:T(8,128)(2,1)S(1)} collective-permute-done((bf16[128,640]{1,0:T(8,128)(2,1)S(1)}, bf16[128,640]{1,0:T(8,128)(2,1)S(1)}, u32[]{:S(2)}, u32[]{:S(2)}) %collective-permute-start.29) | collective-permute-done | bytes 163872 | tf_op jit(solution)/shard_map/ppermute | solution.py:33
  101.1 2.4 %shard_map.275 = (bf16[128,640]{1,0:T(8,128)(2,1)}, bf16[128,640]{1,0:T(8,128)(2,1)}, f32[1,640]{1,0:T(1,128)}) custom-call(f32[256,640]{1,0:T(8,128)} %get-tuple-element.106.keep, bf16[256,640]{1,0:T(8,128)(2,1)} %copy-done.22, f32[128,640]{1,0:T(8,128)} %get-tuple-element.108.resid, bf16[128,640]{1,0:T(8,128)(2,1)} %bitcast.48, ...), custom_call_target="tpu_custom_call" | custom-call | tf_op jit(solution)/shard_map/pallas_call | solution.py:83
  103.9 5.1 %collective-permute-done.31.refs_2_ = bf16[128,640]{1,0:T(8,128)(2,1)S(1)} collective-permute-done((bf16[128,640]{1,0:T(8,128)(2,1)}, bf16[128,640]{1,0:T(8,128)(2,1)S(1)}, u32[]{:S(2)}, u32[]{:S(2)}) %collective-permute-start.31) | collective-permute-done | bytes 163872 | tf_op jit(solution)/shard_map/ppermute | solution.py:33
  111.1 5.0 %shard_map.276 = (bf16[512,640]{1,0:T(8,128)(2,1)}, bf16[512,512]{1,0:T(8,128)(2,1)}, bf16[512,512]{1,0:T(8,128)(2,1)}, f32[256,640]{1,0:T(8,128)}, bf16[256,640]{1,0:T(8,128)(2,1)}) custom-call(bf16[512,640]{1,0:T(8,128)(2,1)} %get-tuple-element.110.wg, bf16[512,640]{1,0:T(8,128)(2,1)} %get-tuple-element.111.wu, bf16[512,640]{1,0:T(8,128)(2,1)} %get-tuple-element.112.wd, ...), custom_call_target="tpu_custom_call" | custom-call | tf_op jit(solution)/shard_map/pallas_call | solution.py:83
  119.6 5.7 %collective-permute-done.34.refs_0_ = bf16[128,640]{1,0:T(8,128)(2,1)S(1)} collective-permute-done((bf16[128,640]{1,0:T(8,128)(2,1)S(1)}, bf16[128,640]{1,0:T(8,128)(2,1)S(1)}, u32[]{:S(2)}, u32[]{:S(2)}) %collective-permute-start.34) | collective-permute-done | bytes 163872 | tf_op jit(solution)/shard_map/ppermute | solution.py:33
  126.1 4.9 %shard_map.277 = (f32[128,640]{1,0:T(8,128)}, bf16[128,640]{1,0:T(8,128)(2,1)}, f32[128,1024]{1,0:T(8,128)}, f32[256,512]{1,0:T(8,128)}, bf16[256,512]{1,0:T(8,1...) custom-call(f32[256,640]{1,0:T(8,128)} %get-tuple-element.116.keep, bf16[256,640]{1,0:T(8,128)(2,1)} %copy-done.23, ...), custom_call_target="tpu_custom_call" | custom-call | tf_op jit(solution)/shard_map/pallas_call | solution.py:83
  130.9 4.3 %shard_map.278 = (bf16[128,1024]{1,0:T(8,128)(2,1)}, f32[1,256]{1,0:T(1,128)}, bf16[1024,640]{1,0:T(8,128)(2,1)}, bf16[1024,640]{1,0:T(8,128)(2,1)}) custom-call(s32[9]{0:T(128)} %stack.100.where, f32[128,1024]{1,0:T(8,128)} %get-tuple-element.125.dqrot, f32[128,1024]{1,0:T(8,128)} %get-tuple-element.126.qraw, f32[8,640]{1,0:T(8,128)} %get-tuple-element.103.gains, ...), custom_call_target="tpu_custom_call" | custom-call | tf_op jit(solution)/shard_map/pallas_call | solution.py:83
  135.2 3.2 %collective-permute-done.37.gave = bf16[1024,640]{1,0:T(8,128)(2,1)S(1)} collective-permute-done((bf16[1024,640]{1,0:T(8,128)(2,1)}, bf16[1024,640]{1,0:T(8,128)(2,1)S(1)}, u32[]{:S(2)}, u32[]{:S(2)}) %collective-permute-start.37) | collective-permute-done | bytes 1310752 | tf_op jit(solution)/shard_map/ppermute | solution.py:33
  139.5 3.2 %shard_map.280 = (f32[512,640]{1,0:T(8,128)}, bf16[512,640]{1,0:T(8,128)(2,1)}) custom-call(s32[1]{0:T(128)} %bitcast.33.outer, bf16[1024,640]{1,0:T(8,128)(2,1)} %get-tuple-element.140.keep, bf16[1024,640]{1,0:T(8,128)(2,1)} %copy-done.3), custom_call_target="tpu_custom_call" | custom-call | tf_op jit(solution)/shard_map/pallas_call | solution.py:83
  143.2 4.6 %shard_map.286 = (bf16[768,640]{1,0:T(8,128)(2,1)}, bf16[768,640]{1,0:T(8,128)(2,1)}) custom-call(bf16[512,640]{1,0:T(8,128)(2,1)} %get-tuple-element.161.nm, bf16[512,640]{1,0:T(8,128)(2,1)} %get-tuple-element.162.dall, bf16[512,512]{1,0:T(8,128)(2,1)} %get-tuple-element.163.dgate, bf16[512,512]{1,0:T(8,128)(2,1)} %get-tuple-element.164.dup, ...), custom_call_target="tpu_custom_call" | custom-call | tf_op jit(solution)/shard_map/pallas_call | solution.py:83
  149.9 12.6 %collective-permute-done.36.refs_0_ = bf16[128,512]{1,0:T(8,128)(2,1)S(1)} collective-permute-done((bf16[128,512]{1,0:T(8,128)(2,1)S(1)}, bf16[128,512]{1,0:T(8,128)(2,1)S(1)}, u32[]{:S(2)}, u32[]{:S(2)}) %collective-permute-start.36) | collective-permute-done | bytes 131104 | tf_op jit(solution)/shard_map/ppermute | solution.py:33
  163.2 4.0 %shard_map.279 = (f32[128,640]{1,0:T(8,128)}, f32[264,640]{1,0:T(8,128)}, bf16[264,640]{1,0:T(8,128)(2,1)}) custom-call(s32[9]{0:T(128)} %stack.100.where, f32[256,512]{1,0:T(8,128)} %get-tuple-element.121.kkeep, bf16[256,512]{1,0:T(8,128)(2,1)} %copy-done.25, f32[128,256]{1,0:T(8,128)} %get-tuple-element.123.kraw, f32[8,640]{1,0:T(8,128)} %get-tuple-element.103.gains, ...), custom_call_target="tpu_custom_call" | custom-call | tf_op jit(solution)/shard_map/pallas_call | solution.py:83
  169.9 2.3 collective-permute-done.53.gave
  172.2 2.6 %shard_map.287 = (f32[192,640]{1,0:T(8,128)}, bf16[192,640]{1,0:T(8,128)(2,1)}, bf16[192,640]{1,0:T(8,128)(2,1)}, bf16[192,640]{1,0:T(8,128)(2,1)}) custom-call(bf16[768,640]{1,0:T(8,128)(2,1)} %get-tuple-element.166.keep, bf16[768,640]{1,0:T(8,128)(2,1)} %collective-permute-done.53.gave), custom_call_target="tpu_custom_call" | custom-call | tf_op jit(solution)/shard_map/pallas_call | solution.py:83
  177.6 2.0 shard_map.283
  186.8 12.8 %collective-permute-done.55 = bf16[192,640]{1,0:T(8,128)(2,1)} collective-permute-done((bf16[192,640]{1,0:T(8,128)(2,1)}, bf16[192,640]{1,0:T(8,128)(2,1)}, u32[]{:S(2)}, u32[]{:S(2)}) %collective-permute-start.55) | collective-permute-done | bytes 245792 | tf_op jit(solution)/shard_map/ppermute | solution.py:33
  204.8 3.8 %collective-permute-start.48 = (bf16[40,640]{1,0:T(8,128)(2,1)}, bf16[40,640]{1,0:T(8,128)(2,1)S(1)}, u32[]{:S(2)}, u32[]{:S(2)}) collective-permute-start(bf16[40,640]{1,0:T(8,128)(2,1)} %get-tuple-element.155), channel_id=1, source_target_pairs={{0,24},{4,28},{8,0},{12,4},{16,8},{20,12},{24,16},{28,20},{1,25},{... | collective-permute-start | bytes 153608 | tf_op jit(solution)/shard_map/ppermute | solution.py:33
  211.1 2.7 %collective-permute-done.49 = bf16[40,640]{1,0:T(8,128)(2,1)S(1)} collective-permute-done((bf16[40,640]{1,0:T(8,128)(2,1)}, bf16[40,640]{1,0:T(8,128)(2,1)S(1)}, u32[]{:S(2)}, u32[]{:S(2)}) %collective-permute-start.49) | collective-permute-done | bytes 51232 | tf_op jit(solution)/shard_map/ppermute | solution.py:33
  217.3 2.6 %collective-permute-done.51 = bf16[40,640]{1,0:T(8,128)(2,1)S(1)} collective-permute-done((bf16[40,640]{1,0:T(8,128)(2,1)S(1)}, bf16[40,640]{1,0:T(8,128)(2,1)S(1)}, u32[]{:S(2)}, u32[]{:S(2)}) %collective-permute-start.51) | collective-permute-done | bytes 51232 | tf_op jit(solution)/shard_map/ppermute | solution.py:33
  224.8 2.9 %shard_map.288 = (f32[640,256]{1,0:T(8,128)}, f32[640,256]{1,0:T(8,128)}, f32[256,640]{1,0:T(8,128)}) custom-call(s32[4]{0:T(128)} %pad_add_fusion.1.where, bf16[192,640]{1,0:T(8,128)(2,1)} %copy-done.5, bf16[192,640]{1,0:T(8,128)(2,1)} %copy-done.36, bf16[192,640]{1,0:T(8,128)(2,1)} %copy-done.30, bf16[192,640]{1,0:T(8,128)(2,1)} %copy-done.38), custom_call_target="tpu_custom_call" | custom-call | tf_op jit(solution)/shard_map/pallas_call | solution.py:83
  (271 shorter events, 78.7 us)
Async XLA Ops:
  4.7 12.5 %collective-permute-start.14 = (bf16[168,640]{1,0:T(8,128)(2,1)S(1)}, bf16[168,640]{1,0:T(8,128)(2,1)S(1)}, u32[]{:S(2)}, u32[]{:S(2)}) collective-permute-start(bf16[168,640]{1,0:T(8,128)(2,1)S(1)} %pad_maximum_fusion.1.refs_0_), channel_id=1, source_target_pairs={{0,1},{1,0},{2,3},{3,2},{4,5},{5,4},{6,7},{7,6},{8,9},{9,8},{10,11... | collective-permute-start | bytes 645128 | tf_op jit(solution)/shard_map/ppermute | solution.py:33
  5.3 12.5 %collective-permute-start.10 = (bf16[168,640]{1,0:T(8,128)(2,1)S(1)}, bf16[168,640]{1,0:T(8,128)(2,1)S(1)}, u32[]{:S(2)}, u32[]{:S(2)}) collective-permute-start(bf16[168,640]{1,0:T(8,128)(2,1)S(1)} %pad_maximum_fusion.1.refs_0_), channel_id=1, source_target_pairs={{0,4},{4,0},{8,12},{12,8},{16,20},{20,16},{24,28},{28,24},{1,5},{5... | collective-permute-start | bytes 645128 | tf_op jit(solution)/shard_map/ppermute | solution.py:33
  11.4 18.6 %collective-permute-start.1 = (bf16[168,640]{1,0:T(8,128)(2,1)S(1)}, bf16[168,640]{1,0:T(8,128)(2,1)S(1)}, u32[]{:S(2)}, u32[]{:S(2)}) collective-permute-start(bf16[168,640]{1,0:T(8,128)(2,1)S(1)} %pad_maximum_fusion.1.refs_0_), channel_id=1, source_target_pairs={{0,16},{4,20},{8,24},{12,28},{16,0},{20,4},{24,8},{28,12},{1,17},{... | collective-permute-start | bytes 645128 | tf_op jit(solution)/shard_map/ppermute | solution.py:33
  11.4 19.1 %collective-permute-start = (bf16[168,640]{1,0:T(8,128)(2,1)S(1)}, bf16[168,640]{1,0:T(8,128)(2,1)S(1)}, u32[]{:S(2)}, u32[]{:S(2)}) collective-permute-start(bf16[168,640]{1,0:T(8,128)(2,1)S(1)} %pad_maximum_fusion.1.refs_0_), channel_id=1, source_target_pairs={{0,8},{4,12},{8,16},{12,20},{16,24},{20,28},{24,0},{28,4},{1,9},{5... | collective-permute-start | bytes 645128 | tf_op jit(solution)/shard_map/ppermute | solution.py:33
  17.2 15.0 %collective-permute-start.20 = (bf16[168,640]{1,0:T(8,128)(2,1)S(1)}, bf16[168,640]{1,0:T(8,128)(2,1)S(1)}, u32[]{:S(2)}, u32[]{:S(2)}) collective-permute-start(bf16[168,640]{1,0:T(8,128)(2,1)S(1)} %collective-permute-done.2.refs_6_), channel_id=1, source_target_pairs={{0,1},{1,0},{2,3},{3,2},{4,5},{5,4},{6,7},{7,6},{8,9},{9,8},{10,11... | collective-permute-start | bytes 645128 | tf_op jit(solution)/shard_map/ppermute | solution.py:33
  17.2 15.5 %collective-permute-start.13 = (bf16[168,640]{1,0:T(8,128)(2,1)S(1)}, bf16[168,640]{1,0:T(8,128)(2,1)S(1)}, u32[]{:S(2)}, u32[]{:S(2)}) collective-permute-start(bf16[168,640]{1,0:T(8,128)(2,1)S(1)} %collective-permute-done.2.refs_6_), channel_id=1, source_target_pairs={{0,4},{4,0},{8,12},{12,8},{16,20},{20,16},{24,28},{28,24},{1,5},{5... | collective-permute-start | bytes 645128 | tf_op jit(solution)/shard_map/ppermute | solution.py:33
  17.8 14.3 %collective-permute-start.15 = (bf16[168,640]{1,0:T(8,128)(2,1)S(1)}, bf16[168,640]{1,0:T(8,128)(2,1)S(1)}, u32[]{:S(2)}, u32[]{:S(2)}) collective-permute-start(bf16[168,640]{1,0:T(8,128)(2,1)S(1)} %collective-permute-done.10.refs_1_), channel_id=1, source_target_pairs={{0,1},{1,0},{2,3},{3,2},{4,5},{5,4},{6,7},{7,6},{8,9},{9,8},{10,11... | collective-permute-start | bytes 645128 | tf_op jit(solution)/shard_map/ppermute | solution.py:33
  30.6 10.6 %collective-permute-start.11 = (bf16[168,640]{1,0:T(8,128)(2,1)S(1)}, bf16[168,640]{1,0:T(8,128)(2,1)S(1)}, u32[]{:S(2)}, u32[]{:S(2)}) collective-permute-start(bf16[168,640]{1,0:T(8,128)(2,1)S(1)} %collective-permute-done.refs_2_), channel_id=1, source_target_pairs={{0,4},{4,0},{8,12},{12,8},{16,20},{20,16},{24,28},{28,24},{1,5},{5... | collective-permute-start | bytes 645128 | tf_op jit(solution)/shard_map/ppermute | solution.py:33
  32.1 10.0 %collective-permute-start.18 = (bf16[168,640]{1,0:T(8,128)(2,1)S(1)}, bf16[168,640]{1,0:T(8,128)(2,1)S(1)}, u32[]{:S(2)}, u32[]{:S(2)}) collective-permute-start(bf16[168,640]{1,0:T(8,128)(2,1)S(1)} %collective-permute-done.1.refs_4_), channel_id=1, source_target_pairs={{0,1},{1,0},{2,3},{3,2},{4,5},{5,4},{6,7},{7,6},{8,9},{9,8},{10,11... | collective-permute-start | bytes 645128 | tf_op jit(solution)/shard_map/ppermute | solution.py:33
  50.5 14.3 %collective-permute-start.8 = (bf16[192,640]{1,0:T(8,128)(2,1)S(1)}, bf16[192,640]{1,0:T(8,128)(2,1)S(1)}, u32[]{:S(2)}, u32[]{:S(2)}) collective-permute-start(bf16[192,640]{1,0:T(8,128)(2,1)S(1)} %pad_maximum_fusion.refs_0_), channel_id=1, source_target_pairs={{0,24},{4,28},{8,0},{12,4},{16,8},{20,12},{24,16},{28,20},{1,25},{... | collective-permute-start | bytes 737288 | tf_op jit(solution)/shard_map/ppermute | solution.py:33
  50.5 21.7 %collective-permute-start.6 = (bf16[192,640]{1,0:T(8,128)(2,1)S(1)}, bf16[192,640]{1,0:T(8,128)(2,1)S(1)}, u32[]{:S(2)}, u32[]{:S(2)}) collective-permute-start(bf16[192,640]{1,0:T(8,128)(2,1)S(1)} %pad_maximum_fusion.refs_0_), channel_id=1, source_target_pairs={{0,16},{4,20},{8,24},{12,28},{16,0},{20,4},{24,8},{28,12},{1,17},{... | collective-permute-start | bytes 737288 | tf_op jit(solution)/shard_map/ppermute | solution.py:33
  50.6 22.2 %collective-permute-start.4 = (bf16[192,640]{1,0:T(8,128)(2,1)S(1)}, bf16[192,640]{1,0:T(8,128)(2,1)S(1)}, u32[]{:S(2)}, u32[]{:S(2)}) collective-permute-start(bf16[192,640]{1,0:T(8,128)(2,1)S(1)} %pad_maximum_fusion.refs_0_), channel_id=1, source_target_pairs={{0,8},{4,12},{8,16},{12,20},{16,24},{20,28},{24,0},{28,4},{1,9},{5... | collective-permute-start | bytes 737288 | tf_op jit(solution)/shard_map/ppermute | solution.py:33
  53.9 20.4 %collective-permute-start.3 = (bf16[192,640]{1,0:T(8,128)(2,1)S(1)}, bf16[192,640]{1,0:T(8,128)(2,1)S(1)}, u32[]{:S(2)}, u32[]{:S(2)}) collective-permute-start(bf16[192,640]{1,0:T(8,128)(2,1)S(1)} %pad_maximum_fusion.refs_0_), channel_id=1, source_target_pairs={{0,4},{4,0},{8,12},{12,8},{16,20},{20,16},{24,28},{28,24},{1,5},{5... | collective-permute-start | bytes 737288 | tf_op jit(solution)/shard_map/ppermute | solution.py:33
  63.2 11.1 %collective-permute-start.26 = (bf16[128,640]{1,0:T(8,128)(2,1)}, bf16[128,640]{1,0:T(8,128)(2,1)S(1)}, u32[]{:S(2)}, u32[]{:S(2)}) collective-permute-start(bf16[128,640]{1,0:T(8,128)(2,1)} %get-tuple-element.105.refs_8_), channel_id=1, source_target_pairs={{0,2},{1,3},{2,0},{3,1},{4,6},{5,7},{6,4},{7,5},{8,10},{9,11},{10,... | collective-permute-start | bytes 491528 | tf_op jit(solution)/shard_map/ppermute | solution.py:33
  64.8 10.1 %collective-permute-start.9 = (bf16[192,640]{1,0:T(8,128)(2,1)S(1)}, bf16[192,640]{1,0:T(8,128)(2,1)S(1)}, u32[]{:S(2)}, u32[]{:S(2)}) collective-permute-start(bf16[192,640]{1,0:T(8,128)(2,1)S(1)} %collective-permute-done.8.refs_6_), channel_id=1, source_target_pairs={{0,4},{4,0},{8,12},{12,8},{16,20},{20,16},{24,28},{28,24},{1,5},{5... | collective-permute-start | bytes 737288 | tf_op jit(solution)/shard_map/ppermute | solution.py:33
  72.8 12.3 %collective-permute-start.5 = (bf16[192,640]{1,0:T(8,128)(2,1)S(1)}, bf16[192,640]{1,0:T(8,128)(2,1)S(1)}, u32[]{:S(2)}, u32[]{:S(2)}) collective-permute-start(bf16[192,640]{1,0:T(8,128)(2,1)S(1)} %collective-permute-done.4.refs_2_), channel_id=1, source_target_pairs={{0,4},{4,0},{8,12},{12,8},{16,20},{20,16},{24,28},{28,24},{1,5},{5... | collective-permute-start | bytes 737288 | tf_op jit(solution)/shard_map/ppermute | solution.py:33
  74.3 10.8 %collective-permute-start.25 = (bf16[128,640]{1,0:T(8,128)(2,1)}, bf16[128,640]{1,0:T(8,128)(2,1)S(1)}, u32[]{:S(2)}, u32[]{:S(2)}) collective-permute-start(bf16[128,640]{1,0:T(8,128)(2,1)} %get-tuple-element.105.refs_8_), channel_id=1, source_target_pairs={{0,1},{1,0},{2,3},{3,2},{4,5},{5,4},{6,7},{7,6},{8,9},{9,8},{10,11... | collective-permute-start | bytes 491528 | tf_op jit(solution)/shard_map/ppermute | solution.py:33
  74.3 10.8 %collective-permute-start.27 = (bf16[128,640]{1,0:T(8,128)(2,1)S(1)}, bf16[128,640]{1,0:T(8,128)(2,1)S(1)}, u32[]{:S(2)}, u32[]{:S(2)}) collective-permute-start(bf16[128,640]{1,0:T(8,128)(2,1)S(1)} %collective-permute-done.26.refs_10_), channel_id=1, source_target_pairs={{0,1},{1,0},{2,3},{3,2},{4,5},{5,4},{6,7},{7,6},{8,9},{9,8},{10,11... | collective-permute-start | bytes 491528 | tf_op jit(solution)/shard_map/ppermute | solution.py:33
  142.7 24.5 %collective-permute-start.38 = (bf16[512,640]{1,0:T(8,128)(2,1)}, bf16[512,640]{1,0:T(8,128)(2,1)S(1)}, u32[]{:S(2)}, u32[]{:S(2)}) collective-permute-start(bf16[512,640]{1,0:T(8,128)(2,1)} %get-tuple-element.143), channel_id=1, source_target_pairs={{0,2},{1,3},{2,0},{3,1},{4,6},{5,7},{6,4},{7,5},{8,10},{9,11},{10,... | collective-permute-start | bytes 1966088 | tf_op jit(solution)/shard_map/ppermute | solution.py:33
  147.8 24.5 %collective-permute-start.53 = (bf16[768,640]{1,0:T(8,128)(2,1)}, bf16[768,640]{1,0:T(8,128)(2,1)}, u32[]{:S(2)}, u32[]{:S(2)}) collective-permute-start(bf16[768,640]{1,0:T(8,128)(2,1)} %get-tuple-element.167), channel_id=1, source_target_pairs={{0,4},{4,0},{8,12},{12,8},{16,20},{20,16},{24,28},{28,24},{1,5},{5... | collective-permute-start | bytes 2949128 | tf_op jit(solution)/shard_map/ppermute | solution.py:33
  148.3 14.1 %collective-permute-start.36 = (bf16[128,512]{1,0:T(8,128)(2,1)S(1)}, bf16[128,512]{1,0:T(8,128)(2,1)S(1)}, u32[]{:S(2)}, u32[]{:S(2)}) collective-permute-start(bf16[128,512]{1,0:T(8,128)(2,1)S(1)} %add_convert_fusion.3), channel_id=1, source_target_pairs={{0,2},{1,3},{2,0},{3,1},{4,6},{5,7},{6,4},{7,5},{8,10},{9,11},{10,... | collective-permute-start | bytes 393224 | tf_op jit(solution)/shard_map/ppermute | solution.py:33
  169.3 12.6 %collective-permute-start.39 = (bf16[256,640]{1,0:T(8,128)(2,1)S(1)}, bf16[256,640]{1,0:T(8,128)(2,1)S(1)}, u32[]{:S(2)}, u32[]{:S(2)}) collective-permute-start(bf16[256,640]{1,0:T(8,128)(2,1)S(1)} %slice.49), channel_id=1, source_target_pairs={{0,4},{4,0},{8,12},{12,8},{16,20},{20,16},{24,28},{28,24},{1,5},{5... | collective-permute-start | bytes 983048 | tf_op jit(solution)/shard_map/ppermute | solution.py:33
  174.8 11.6 %collective-permute-start.54 = (bf16[192,640]{1,0:T(8,128)(2,1)}, bf16[192,640]{1,0:T(8,128)(2,1)S(1)}, u32[]{:S(2)}, u32[]{:S(2)}) collective-permute-start(bf16[192,640]{1,0:T(8,128)(2,1)} %get-tuple-element.169), channel_id=1, source_target_pairs={{0,24},{4,28},{8,0},{12,4},{16,8},{20,12},{24,16},{28,20},{1,25},{... | collective-permute-start | bytes 737288 | tf_op jit(solution)/shard_map/ppermute | solution.py:33
  174.8 24.7 %collective-permute-start.55 = (bf16[192,640]{1,0:T(8,128)(2,1)}, bf16[192,640]{1,0:T(8,128)(2,1)}, u32[]{:S(2)}, u32[]{:S(2)}) collective-permute-start(bf16[192,640]{1,0:T(8,128)(2,1)} %get-tuple-element.170), channel_id=1, source_target_pairs={{0,16},{4,20},{8,24},{12,28},{16,0},{20,4},{24,8},{28,12},{1,17},{... | collective-permute-start | bytes 737288 | tf_op jit(solution)/shard_map/ppermute | solution.py:33
  174.8 24.7 %collective-permute-start.56 = (bf16[192,640]{1,0:T(8,128)(2,1)}, bf16[192,640]{1,0:T(8,128)(2,1)}, u32[]{:S(2)}, u32[]{:S(2)}) collective-permute-start(bf16[192,640]{1,0:T(8,128)(2,1)} %get-tuple-element.171), channel_id=1, source_target_pairs={{0,8},{4,12},{8,16},{12,20},{16,24},{20,28},{24,0},{28,4},{1,9},{5... | collective-permute-start | bytes 737288 | tf_op jit(solution)/shard_map/ppermute | solution.py:33
  179.6 22.8 %collective-permute-start.47 = (bf16[136,640]{1,0:T(8,128)(2,1)}, bf16[136,640]{1,0:T(8,128)(2,1)S(1)}, u32[]{:S(2)}, u32[]{:S(2)}) collective-permute-start(bf16[136,640]{1,0:T(8,128)(2,1)} %get-tuple-element.153), channel_id=1, source_target_pairs={{0,4},{4,0},{8,12},{12,8},{16,20},{20,16},{24,28},{28,24},{1,5},{5... | collective-permute-start | bytes 522248 | tf_op jit(solution)/shard_map/ppermute | solution.py:33
  184.6 24.0 %collective-permute-start.40 = (bf16[64,640]{1,0:T(8,128)(2,1)}, bf16[64,640]{1,0:T(8,128)(2,1)S(1)}, u32[]{:S(2)}, u32[]{:S(2)}) collective-permute-start(bf16[64,640]{1,0:T(8,128)(2,1)} %get-tuple-element.145), channel_id=1, source_target_pairs={{0,24},{4,28},{8,0},{12,4},{16,8},{20,12},{24,16},{28,20},{1,25},{... | collective-permute-start | bytes 245768 | tf_op jit(solution)/shard_map/ppermute | solution.py:33
  186.5 22.1 %collective-permute-start.41 = (bf16[64,640]{1,0:T(8,128)(2,1)}, bf16[64,640]{1,0:T(8,128)(2,1)S(1)}, u32[]{:S(2)}, u32[]{:S(2)}) collective-permute-start(bf16[64,640]{1,0:T(8,128)(2,1)} %get-tuple-element.146), channel_id=1, source_target_pairs={{0,16},{4,20},{8,24},{12,28},{16,0},{20,4},{24,8},{28,12},{1,17},{... | collective-permute-start | bytes 245768 | tf_op jit(solution)/shard_map/ppermute | solution.py:33
  199.6 11.0 %collective-permute-start.42 = (bf16[64,640]{1,0:T(8,128)(2,1)}, bf16[64,640]{1,0:T(8,128)(2,1)S(1)}, u32[]{:S(2)}, u32[]{:S(2)}) collective-permute-start(bf16[64,640]{1,0:T(8,128)(2,1)} %get-tuple-element.147), channel_id=1, source_target_pairs={{0,8},{4,12},{8,16},{12,20},{16,24},{20,28},{24,0},{28,4},{1,9},{5... | collective-permute-start | bytes 245768 | tf_op jit(solution)/shard_map/ppermute | solution.py:33
  200.8 15.5 %collective-permute-start.58 = (bf16[192,640]{1,0:T(8,128)(2,1)S(1)}, bf16[192,640]{1,0:T(8,128)(2,1)S(1)}, u32[]{:S(2)}, u32[]{:S(2)}) collective-permute-start(bf16[192,640]{1,0:T(8,128)(2,1)S(1)} %add_convert_fusion.refs_0_), channel_id=1, source_target_pairs={{0,2},{1,3},{2,0},{3,1},{4,6},{5,7},{6,4},{7,5},{8,10},{9,11},{10,... | collective-permute-start | bytes 737288 | tf_op jit(solution)/shard_map/ppermute | solution.py:33
  216.8 10.9 %collective-permute-start.43 = (bf16[64,640]{1,0:T(8,128)(2,1)S(1)}, bf16[64,640]{1,0:T(8,128)(2,1)S(1)}, u32[]{:S(2)}, u32[]{:S(2)}) collective-permute-start(bf16[64,640]{1,0:T(8,128)(2,1)S(1)} %add_convert_fusion.4.refs_0_), channel_id=1, source_target_pairs={{0,1},{1,0},{2,3},{3,2},{4,5},{5,4},{6,7},{7,6},{8,9},{9,8},{10,11... | collective-permute-start | bytes 245768 | tf_op jit(solution)/shard_map/ppermute | solution.py:33
  216.8 10.8 %collective-permute-start.45 = (bf16[64,640]{1,0:T(8,128)(2,1)S(1)}, bf16[64,640]{1,0:T(8,128)(2,1)S(1)}, u32[]{:S(2)}, u32[]{:S(2)}) collective-permute-start(bf16[64,640]{1,0:T(8,128)(2,1)S(1)} %collective-permute-done.44.refs_2_), channel_id=1, source_target_pairs={{0,1},{1,0},{2,3},{3,2},{4,5},{5,4},{6,7},{7,6},{8,9},{9,8},{10,11... | collective-permute-start | bytes 245768 | tf_op jit(solution)/shard_map/ppermute | solution.py:33
  (91 other events, 683.7 us)
